TPU v7x, 32 devices: a whole 2x2x4 slice. The times are simulated.
32 devices in a mesh: solver: 8 (over y, x, core), group: 4 (over z).
Axes of the slice: x: 2, y: 2, z: 4, core: 2. Of those that a mesh axis runs over, the one named last changes fastest.
Arguments:
- field: float32 [8, 8, 8, 8192], P(None, None, None, ('solver', 'group')), may hold values from -6 to 6
- first_weight: bfloat16 [8, 1024], replicated, may hold values from -2 to 2
- second_weight: bfloat16 [1024, 1], replicated, may hold values from -0.1875 to 0.1875
- face_edges: int32 [2, 256], replicated, may hold values from 0 to 63, as said below
- sample_index: int32 [2048], P(('solver', 'group')), may hold values from 0 to 31
- route: int32 [2048, 1], P(('solver', 'group')), may hold values from 0 to 7; in each aligned block of 64 rows (0 to 63, 64 to 127, ...) at most 16 rows name the same one
Outputs:
- new_field: float32 [8, 8, 8, 8192], P(None, None, None, ('solver', 'group'))
- new_first: bfloat16 [8, 1024], replicated
- new_second: bfloat16 [1024, 1], replicated
Inputs may be any that keep to these rules, and one draw needn't show every extreme that they name: `sample_index`: indices of wall elements (ey = 0) of the sample's own device, in the order ex * 8 + ez; they may repeat. `route`: at most 16 of the samples of one device name one learner, a bound that some block reaches by some device in every draw. `face_edges`: no edge joins a node to itself; edges may repeat.
All inputs are finite; a program needn't handle non-finite values.
Results may differ from a plain program's by a relative error of at most 0.001.
The roundings to bfloat16 on the way count: a program that leaves them out, or rounds other values in their place, can miss the bound.
Values sent between devices are 32-bit elements; how exact they have to be, the bound alone decides.
A program may use at most 128 MiB of HBM per device.

v0:
```python
import jax
import jax.numpy as jnp
import numpy as np
from jax import lax
from jax.sharding import PartitionSpec as P

FLOW_STEPS = 5
EXL = 4
EZL = 8
EY = 8


HIGH = lax.Precision.HIGHEST
TIME_STEP = 0.002
VISCOSITY = 0.01
VELOCITY = 1.0
PENALTY = 1.0
STRESS_SCALE = 0.1
LEARN_RATE = 0.05


def with_halo(block, sides, width):
    for axis, dim in sides:
        count = lax.axis_size(axis)
        forward = [(i, i + 1) for i in range(count - 1)]
        forward.append((count - 1, 0))
        backward = [(target, source) for source, target in forward]
        low = lax.ppermute(
            lax.slice_in_dim(block, block.shape[dim] - width, None, axis=dim), axis, forward
        )
        high = lax.ppermute(lax.slice_in_dim(block, 0, width, axis=dim), axis, backward)
        block = jnp.concatenate([low, block, high], axis=dim)
    return block


def legendre_table(points_x, points):
    table = np.zeros((points_x.shape[0], points))
    table[:, 0] = 1.0
    table[:, 1] = points_x
    for degree in range(2, points):
        table[:, degree] = (
            (2 * degree - 1) * points_x * table[:, degree - 1] - (degree - 1) * table[:, degree - 2]
        ) / degree
    return table


def gll_tables(points):
    order = points - 1
    guess = np.cos(np.pi * np.arange(points) / order)
    for sweep in range(100):
        table = legendre_table(guess, points)
        guess = guess - (guess * table[:, order] - table[:, order - 1]) / (points * table[:, order])
    nodes = guess[::-1]
    values = legendre_table(nodes, points)[:, order]
    matrix = np.zeros((points, points))
    for row in range(points):
        for column in range(points):
            if row != column:
                matrix[row, column] = values[row] / (values[column] * (nodes[row] - nodes[column]))
    matrix[0, 0] = -order * (order + 1) / 4.0
    matrix[order, order] = order * (order + 1) / 4.0
    return (jnp.asarray(matrix, jnp.float32), 2.0 / (order * (order + 1)))


def face_adjacency(face_edges, nodes):
    columns = jnp.arange(nodes, dtype=jnp.int32)
    source = (face_edges[0][:, None] == columns[None, :]).astype(jnp.float32)
    target = (face_edges[1][:, None] == columns[None, :]).astype(jnp.float32)
    single = jnp.dot(source.T, target, precision=HIGH)
    tile = 128 // nodes
    return (0.25 * jnp.kron(jnp.eye(tile, dtype=jnp.float32), single)).astype(jnp.bfloat16)


def network_output(first_weight, second_weight, adjacency, features):
    width = first_weight.shape[1]
    tile = adjacency.shape[0]
    inputs = jnp.transpose(features, (1, 0, 2)).reshape(features.shape[1], -1)
    before = jnp.dot(first_weight.T, inputs, preferred_element_type=jnp.float32)
    hidden = jnp.maximum(before, 0.0).astype(jnp.bfloat16)
    spread = jnp.einsum(
        "hbn,nm->hbm",
        hidden.reshape(width, -1, tile),
        adjacency,
        preferred_element_type=jnp.float32,
    ).reshape(width, -1)
    mixed = (hidden.astype(jnp.float32) + spread).astype(jnp.bfloat16)
    output = jnp.dot(second_weight.T, mixed, preferred_element_type=jnp.float32)
    return (inputs, before, mixed, output)


def block_grads(first_weight, second_weight, adjacency, features, target, share):
    width = first_weight.shape[1]
    tile = adjacency.shape[0]
    inputs, before, mixed, output = network_output(first_weight, second_weight, adjacency, features)
    node_share = jnp.repeat(share, features.shape[2])[None, :]
    error = ((output - target.reshape(1, -1).astype(jnp.float32)) * node_share).astype(jnp.bfloat16)
    grad_second = lax.dot_general(
        mixed, error, (((1,), (1,)), ((), ())), preferred_element_type=jnp.float32
    )
    back_mixed = jnp.dot(second_weight, error, preferred_element_type=jnp.float32).astype(
        jnp.bfloat16
    )
    back_spread = jnp.einsum(
        "hbm,nm->hbn",
        back_mixed.reshape(width, -1, tile),
        adjacency,
        preferred_element_type=jnp.float32,
    ).reshape(width, -1)
    back_hidden = jnp.where(before > 0.0, back_mixed.astype(jnp.float32) + back_spread, 0.0).astype(
        jnp.bfloat16
    )
    grad_first = lax.dot_general(
        inputs, back_hidden, (((1,), (1,)), ((), ())), preferred_element_type=jnp.float32
    )
    return (grad_first, grad_second)


def learner_grads(first_weight, second_weight, adjacency, features, target, share):
    group_size = 32
    blocks = features.shape[0] // group_size
    points = features.shape[1]
    face = features.shape[2]

    def one_block(carry, pieces):
        grads = block_grads(first_weight, second_weight, adjacency, pieces[0], pieces[1], pieces[2])
        return ((carry[0] + grads[0], carry[1] + grads[1]), None)

    start = (
        jnp.zeros(first_weight.shape, jnp.float32),
        jnp.zeros(second_weight.shape, jnp.float32),
    )
    pieces = (
        features.reshape(blocks, group_size, points, face),
        target.reshape(blocks, group_size, face),
        share.reshape(blocks, group_size),
    )
    result, unused = lax.scan(one_block, start, pieces)
    return result


def neighbour_faces(field):
    points = field.shape[0]
    last = points - 1
    elements = field.shape[3]
    face = points * points
    faces = jnp.stack([field[0], field[last], field[:, :, 0], field[:, :, last]])
    traces = faces.reshape(4, face, elements).transpose(2, 0, 1).reshape(EXL, EZL, EY * 4 * face)
    padded = with_halo(traces, (("solver", 0), ("group", 1)), 1)
    padded = padded.reshape(EXL + 2, EZL + 2, EY, 4, face)

    def unpack(block):
        return block.reshape(elements, face).T.reshape(points, points, elements)

    before_x = unpack(padded[:EXL, 1 : EZL + 1, :, 1])
    after_x = unpack(padded[2:, 1 : EZL + 1, :, 0])
    before_z = unpack(padded[1 : EXL + 1, :EZL, :, 3])
    after_z = unpack(padded[1 : EXL + 1, 2:, :, 2])
    return (before_x, after_x, before_z, after_z)


def flow_step(field, stress, deriv, second_deriv, gain):
    points = field.shape[0]
    last = points - 1
    elements = field.shape[3]
    along_x = jnp.einsum("ai,ijke->ajke", deriv, field, precision=HIGH)
    curve = (
        jnp.einsum("ai,ijke->ajke", second_deriv, field, precision=HIGH)
        + jnp.einsum("aj,ijke->iake", second_deriv, field, precision=HIGH)
        + jnp.einsum("ak,ijke->ijae", second_deriv, field, precision=HIGH)
    )
    change = -2.0 * VELOCITY * along_x + 4.0 * VISCOSITY * curve
    before_x, after_x, before_z, after_z = neighbour_faces(field)
    lower = field[:, 0].reshape(points, points, EXL * EZL, EY)
    upper = field[:, last].reshape(points, points, EXL * EZL, EY)
    lower_jump = PENALTY * (upper[..., :-1] - lower[..., 1:])
    lower_term = jnp.concatenate([stress[..., None], lower_jump], axis=3).reshape(
        points, points, elements
    )
    above = jnp.concatenate([lower[..., 1:], jnp.zeros_like(lower[..., :1])], axis=3)
    upper_term = (PENALTY * (above - upper)).reshape(points, points, elements)
    change = change.at[0].add(gain * (VELOCITY + PENALTY) * (before_x - field[0]))
    change = change.at[last].add(gain * PENALTY * (after_x - field[last]))
    change = change.at[:, :, 0].add(gain * PENALTY * (before_z - field[:, :, 0]))
    change = change.at[:, :, last].add(gain * PENALTY * (after_z - field[:, :, last]))
    change = change.at[:, 0].add(gain * lower_term)
    change = change.at[:, last].add(gain * upper_term)
    return field + TIME_STEP * change


def shards(field, first_weight, second_weight, face_edges, sample_index, route):
    points = field.shape[0]
    face = points * points
    deriv, end_weight = gll_tables(points)
    second_deriv = jnp.dot(deriv, deriv, precision=HIGH)
    gain = 2.0 / end_weight
    walls = EXL * EZL
    learners = lax.axis_size("solver")
    devices = learners * lax.axis_size("group")
    adjacency = face_adjacency(face_edges, face)
    wall_field = field[..., ::EY]
    features = (
        jnp.transpose(wall_field, (3, 1, 0, 2)).reshape(walls, points, face).astype(jnp.bfloat16)
    )
    slope = jnp.einsum("j,ijkw->wik", deriv[0], wall_field, precision=HIGH)
    target = (STRESS_SCALE * slope).reshape(walls, face).astype(jnp.bfloat16)
    payload = jnp.concatenate([features.reshape(walls, points * face), target], axis=1)
    picked = (sample_index[:, None] == jnp.arange(walls, dtype=jnp.int32)[None, :]).astype(
        jnp.bfloat16
    )
    chosen = jnp.dot(picked, payload, preferred_element_type=jnp.float32).astype(jnp.bfloat16)
    destination = route[:, 0]
    columns = (destination[:, None] == jnp.arange(learners, dtype=jnp.int32)[None, :]).astype(
        jnp.float32
    )
    counts = lax.psum(jnp.sum(columns, axis=0), "solver")
    share = jnp.dot(columns, 1.0 / (jnp.maximum(counts, 1.0) * devices), precision=HIGH)
    sample_features = chosen[:, : points * face].reshape(-1, points, face)
    sample_target = chosen[:, points * face :]
    grad_first, grad_second = learner_grads(
        first_weight, second_weight, adjacency, sample_features, sample_target, share
    )
    grad_first, grad_second = lax.psum((grad_first, grad_second), ("solver", "group"))
    new_first = (first_weight.astype(jnp.float32) - LEARN_RATE * grad_first).astype(jnp.bfloat16)
    new_second = (second_weight.astype(jnp.float32) - LEARN_RATE * grad_second).astype(jnp.bfloat16)
    output = network_output(new_first, new_second, adjacency, features)[3]
    stress = output.reshape(walls, points, points).transpose(1, 2, 0)
    for step in range(FLOW_STEPS):
        field = flow_step(field, stress, deriv, second_deriv, gain)
    return (field, new_first, new_second)


def solution(mesh):
    return jax.shard_map(
        shards,
        mesh=mesh,
        in_specs=(
            P(None, None, None, ("solver", "group")),
            P(),
            P(),
            P(),
            P(("solver", "group")),
            P(("solver", "group"), None),
        ),
        out_specs=(P(None, None, None, ("solver", "group")), P(), P()),
        check_vma=False,
    )
```

profile of v0, /device:TPU:0, one launch (start us, length us, event | category | flops | bytes accessed | tf_op | source)
XLA Modules:
  0.0 353.0 jit_solution(3120314060666266291)
XLA Ops:
  3.9 3.4 collective-permute-start.1
  9.1 2.8 slice.1142
  15.7 14.6 %psum.21 = f32[8]{0:T(128)S(1)} all-reduce(f32[8]{0:T(128)S(1)} %convert_reduce_fusion), channel_id=1, replica_groups=mesh['solver'=8,'group'=4] {'solver'}, use_global_device_ids=true, to_apply=%region_1.2 | all-reduce | flops 8 | bytes 64 | tf_op jit(solution)/shard_map/psum | solution.py:215
  31.6 46.8 %while.43 = (s32[]{:T(128)}, f32[8,1024]{1,0:T(8,128)S(1)}, f32[1024,1]{0,1:T(1,128)S(1)}, bf16[2,32,8,64]{3,2,1,0:T(8,128)(2,1)S(1)}, bf16[8,1024]{1,0:T(8,128)...) while((s32[]{:T(128)}, f32[8,1024]{1,0:T(8,128)S(1)}, ...), condition=%wide.region_3.4_spmd.clone, body=%wide.region_2.3_spmd.clone.sunk | while | flops 1178678272 | bytes 118186584 | solution.py:137
  32.4 4.7 %maximum_convert_fusion.3 = (bf16[2048,1024]{1,0:T(8,128)(2,1)S(1)}, f32[2048,1024]{1,0:T(8,128)}) fusion(bf16[8,2048]{1,0:T(8,128)(2,1)S(1)} %reshape.1396, bf16[8,1024]{1,0:T(8,128)(2,1)S(1)} %get-tuple-element.705), kind=kOutput, calls=%fused_computation.7.clone.1 | convolution fusion | flops 37748736 | bytes 12632064 | tf_op jit(solution)/shard_map/while/body/eval_jaxpr/dot_general | solution.py:78
  37.1 4.9 %fusion.220 = f32[1024,16,128]{0,2,1:T(8,128)} fusion(bf16[1024,16,128]{0,2,1:T(8,128)(2,1)S(1)} %bitcast.396, bf16[128,128]{1,0:T(8,128)(2,1)S(1)} %convert_element_type.195), kind=kOutput, calls=%fused_computation.13.clone.1 | convolution fusion | flops 536870912 | bytes 12615680 | tf_op jit(solution)/shard_map/while/body/eval_jaxpr/hbn,nm->hbm/dot_general | solution.py:80
  41.9 5.0 %fusion.221 = bf16[1024,2048]{0,1:T(8,128)(2,1)S(1)} fusion(f32[1024,16,128]{0,2,1:T(8,128)} %fusion.220, bf16[2048,1024]{1,0:T(8,128)(2,1)S(1)} %get-tuple-element.671), kind=kLoop, calls=%fused_computation.5.clone.1 | loop fusion | flops 6291456 | bytes 16777216 | tf_op jit(solution)/shard_map/while/body/eval_jaxpr/convert_element_type | solution.py:86
  55.8 4.7 %maximum_convert_fusion.3 = (bf16[2048,1024]{1,0:T(8,128)(2,1)S(1)}, f32[2048,1024]{1,0:T(8,128)}) fusion(bf16[8,2048]{1,0:T(8,128)(2,1)S(1)} %reshape.1396, bf16[8,1024]{1,0:T(8,128)(2,1)S(1)} %get-tuple-element.705), kind=kOutput, calls=%fused_computation.7.clone.1 | convolution fusion | flops 37748736 | bytes 12632064 | tf_op jit(solution)/shard_map/while/body/eval_jaxpr/dot_general | solution.py:78
  60.5 4.9 %fusion.220 = f32[1024,16,128]{0,2,1:T(8,128)} fusion(bf16[1024,16,128]{0,2,1:T(8,128)(2,1)S(1)} %bitcast.396, bf16[128,128]{1,0:T(8,128)(2,1)S(1)} %convert_element_type.195), kind=kOutput, calls=%fused_computation.13.clone.1 | convolution fusion | flops 536870912 | bytes 12615680 | tf_op jit(solution)/shard_map/while/body/eval_jaxpr/hbn,nm->hbm/dot_general | solution.py:80
  65.3 5.0 %fusion.221 = bf16[1024,2048]{0,1:T(8,128)(2,1)S(1)} fusion(f32[1024,16,128]{0,2,1:T(8,128)} %fusion.220, bf16[2048,1024]{1,0:T(8,128)(2,1)S(1)} %get-tuple-element.671), kind=kLoop, calls=%fused_computation.5.clone.1 | loop fusion | flops 6291456 | bytes 16777216 | tf_op jit(solution)/shard_map/while/body/eval_jaxpr/convert_element_type | solution.py:86
  78.5 40.0 %all-reduce.5 = (f32[8,1024]{1,0:T(8,128)S(1)}, f32[1024,1]{0,1:T(1,128)S(1)}) all-reduce(f32[8,1024]{1,0:T(8,128)S(1)} %get-tuple-element.412, f32[1024,1]{0,1:T(1,128)S(1)} %get-tuple-element.411), channel_id=1, replica_groups=mesh['solver'=8,'group'=4] {'solver','group'}, use_global_device_ids=true, to_apply=%region_5.6 | all-reduce | flops 9216 | bytes 73728 | tf_op jit(solution)/shard_map/psum | solution.py:222
  125.7 5.1 %fusion.10 = bf16[2048,1024]{0,1:T(8,128)(2,1)} fusion(f32[128,8,16,128]{3,2,1,0:T(8,128)S(1)} %bitcast.401, bf16[1024,2048]{1,0:T(8,128)(2,1)S(1)} %maximum_convert_fusion.1), kind=kLoop, calls=%fused_computation.24 | loop fusion | flops 6291456 | bytes 16777216 | tf_op jit(solution)/shard_map/dot_general | solution.py:87
  130.8 6.8 %copy.403 = bf16[2048,1024]{1,0:T(8,128)(2,1)} copy(bf16[2048,1024]{0,1:T(8,128)(2,1)} %fusion.10) | data formatting | bytes 8388608 | tf_op jit(solution)/shard_map/dot_general | solution.py:87
  137.7 11.6 %fusion.88 = f32[1,32,8,8]{3,0,2,1:T(1,128)S(1)} fusion(bf16[32,8,8,1024]{3,2,1,0:T(8,128)(2,1)} %bitcast.403, bf16[1024,1]{0,1:T(2,128)(2,1)S(1)} %subtract_convert_fusion.1), kind=kOutput, calls=%fused_computation.216 | convolution fusion | flops 4194304 | bytes 4204544 | tf_op jit(solution)/shard_map/dot_general | solution.py:87
  161.2 2.7 fusion.29
  192.0 3.2 fusion.25
  199.9 3.8 %collective-permute-start.7 = (f32[6,1,2048]{2,1,0:T(1,128)S(1)}, f32[6,1,2048]{2,1,0:T(1,128)S(1)}, u32[]{:S(2)}, u32[]{:S(2)}) collective-permute-start(f32[6,1,2048]{2,1,0:T(1,128)S(1)} %get-tuple-element.585), channel_id=1, source_target_pairs={{1,0},{2,1},{3,2},{0,3},{5,4},{6,5},{7,6},{4,7},{9,8},{10,9},{11,1... | collective-permute-start | bytes 147464 | tf_op jit(solution)/shard_map/ppermute | solution.py:31
  203.7 2.5 maximum_multiply_fusion.1
  214.5 2.5 scatter-add.110
  248.5 3.8 %collective-permute-start.11 = (f32[6,1,2048]{2,1,0:T(1,128)S(1)}, f32[6,1,2048]{2,1,0:T(1,128)S(1)}, u32[]{:S(2)}, u32[]{:S(2)}) collective-permute-start(f32[6,1,2048]{2,1,0:T(1,128)S(1)} %get-tuple-element.583), channel_id=1, source_target_pairs={{1,0},{2,1},{3,2},{0,3},{5,4},{6,5},{7,6},{4,7},{9,8},{10,9},{11,1... | collective-permute-start | bytes 147464 | tf_op jit(solution)/shard_map/ppermute | solution.py:31
  252.4 2.5 maximum_multiply_fusion.2
  280.8 3.2 fusion.17
  288.7 3.8 %collective-permute-start.15 = (f32[6,1,2048]{2,1,0:T(1,128)S(1)}, f32[6,1,2048]{2,1,0:T(1,128)S(1)}, u32[]{:S(2)}, u32[]{:S(2)}) collective-permute-start(f32[6,1,2048]{2,1,0:T(1,128)S(1)} %get-tuple-element.581), channel_id=1, source_target_pairs={{1,0},{2,1},{3,2},{0,3},{5,4},{6,5},{7,6},{4,7},{9,8},{10,9},{11,1... | collective-permute-start | bytes 147464 | tf_op jit(solution)/shard_map/ppermute | solution.py:31
  338.0 3.8 %collective-permute-start.19 = (f32[6,1,2048]{2,1,0:T(1,128)}, f32[6,1,2048]{2,1,0:T(1,128)}, u32[]{:S(2)}, u32[]{:S(2)}) collective-permute-start(f32[6,1,2048]{2,1,0:T(1,128)} %get-tuple-element.579), channel_id=1, source_target_pairs={{1,0},{2,1},{3,2},{0,3},{5,4},{6,5},{7,6},{4,7},{9,8},{10,9},{11,1... | collective-permute-start | bytes 147464 | tf_op jit(solution)/shard_map/ppermute | solution.py:31
  (448 shorter events, 204.9 us)
Async XLA Ops:
  0.7 29.9 %copy-start.28 = (s32[2,256]{1,0:T(2,128)S(1)}, s32[2,256]{1,0:T(2,128)}, u32[]{:S(2)}) copy-start(s32[2,256]{1,0:T(2,128)} %param.72) | copy-start | bytes 6148
  2.1 29.5 %copy-start.21 = (bf16[8,1024]{1,0:T(8,128)(2,1)S(1)}, bf16[8,1024]{1,0:T(8,128)(2,1)}, u32[]{:S(2)}) copy-start(bf16[8,1024]{1,0:T(8,128)(2,1)} %param.70) | copy-start | bytes 49156
  2.1 29.5 %copy-start.22 = (bf16[1024,1]{0,1:T(2,128)(2,1)S(1)}, bf16[1024,1]{0,1:T(2,128)(2,1)}, u32[]{:S(2)}) copy-start(bf16[1024,1]{0,1:T(2,128)(2,1)} %param.71) | copy-start | bytes 6148
  2.9 28.7 %copy-start.8 = (f32[256,4,64]{0,2,1:T(8,128)}, f32[256,4,64]{0,2,1:T(8,128)S(1)}, u32[]{:S(2)}) copy-start(f32[256,4,64]{0,2,1:T(8,128)S(1)} %maximum_bitcast_fusion) | copy-start | bytes 786436
  3.9 152.4 %collective-permute-start.1 = (f32[1,8,2048]{2,1,0:T(8,128)}, f32[1,8,2048]{2,1,0:T(8,128)}, u32[]{:S(2)}, u32[]{:S(2)}) collective-permute-start(f32[1,8,2048]{2,1,0:T(8,128)} %slice.1131), channel_id=1, source_target_pairs={{4,0},{8,4},{12,8},{16,12},{20,16},{24,20},{28,24},{0,28},{5,1},{9... | collective-permute-start | bytes 196616 | tf_op jit(solution)/shard_map/ppermute | solution.py:31
  8.2 147.3 %collective-permute-start = (f32[1,8,2048]{2,1,0:T(8,128)}, f32[1,8,2048]{2,1,0:T(8,128)}, u32[]{:S(2)}, u32[]{:S(2)}) collective-permute-start(f32[1,8,2048]{2,1,0:T(8,128)} %slice.1129), channel_id=1, source_target_pairs={{0,4},{4,8},{8,12},{12,16},{16,20},{20,24},{24,28},{28,0},{1,5},{5... | collective-permute-start | bytes 196616 | tf_op jit(solution)/shard_map/ppermute | solution.py:28
  157.3 10.1 %collective-permute-start.2 = (f32[6,1,2048]{2,1,0:T(1,128)S(1)}, f32[6,1,2048]{2,1,0:T(1,128)S(1)}, u32[]{:S(2)}, u32[]{:S(2)}) collective-permute-start(f32[6,1,2048]{2,1,0:T(1,128)S(1)} %get-tuple-element.586), channel_id=1, source_target_pairs={{0,1},{1,2},{2,3},{3,0},{4,5},{5,6},{6,7},{7,4},{8,9},{9,10},{10,1... | collective-permute-start | bytes 147464 | tf_op jit(solution)/shard_map/ppermute | solution.py:28
  158.9 8.5 %collective-permute-start.3 = (f32[6,1,2048]{2,1,0:T(1,128)S(1)}, f32[6,1,2048]{2,1,0:T(1,128)S(1)}, u32[]{:S(2)}, u32[]{:S(2)}) collective-permute-start(f32[6,1,2048]{2,1,0:T(1,128)S(1)} %get-tuple-element.587), channel_id=1, source_target_pairs={{1,0},{2,1},{3,2},{0,3},{5,4},{6,5},{7,6},{4,7},{9,8},{10,9},{11,1... | collective-permute-start | bytes 147464 | tf_op jit(solution)/shard_map/ppermute | solution.py:31
  186.4 12.5 %collective-permute-start.5 = (f32[1,8,2048]{2,1,0:T(8,128)S(1)}, f32[1,8,2048]{2,1,0:T(8,128)S(1)}, u32[]{:S(2)}, u32[]{:S(2)}) collective-permute-start(f32[1,8,2048]{2,1,0:T(8,128)S(1)} %slice.1161), channel_id=1, source_target_pairs={{4,0},{8,4},{12,8},{16,12},{20,16},{24,20},{28,24},{0,28},{5,1},{9... | collective-permute-start | bytes 196616 | tf_op jit(solution)/shard_map/ppermute | solution.py:31
  187.1 11.8 %collective-permute-start.4 = (f32[1,8,2048]{2,1,0:T(8,128)S(1)}, f32[1,8,2048]{2,1,0:T(8,128)S(1)}, u32[]{:S(2)}, u32[]{:S(2)}) collective-permute-start(f32[1,8,2048]{2,1,0:T(8,128)S(1)} %slice.1159), channel_id=1, source_target_pairs={{0,4},{4,8},{8,12},{12,16},{16,20},{20,24},{24,28},{28,0},{1,5},{5... | collective-permute-start | bytes 196616 | tf_op jit(solution)/shard_map/ppermute | solution.py:28
  199.8 8.7 %collective-permute-start.6 = (f32[6,1,2048]{2,1,0:T(1,128)S(1)}, f32[6,1,2048]{2,1,0:T(1,128)S(1)}, u32[]{:S(2)}, u32[]{:S(2)}) collective-permute-start(f32[6,1,2048]{2,1,0:T(1,128)S(1)} %get-tuple-element.584), channel_id=1, source_target_pairs={{0,1},{1,2},{2,3},{3,0},{4,5},{5,6},{6,7},{7,4},{8,9},{9,10},{10,1... | collective-permute-start | bytes 147464 | tf_op jit(solution)/shard_map/ppermute | solution.py:28
  199.9 8.6 %collective-permute-start.7 = (f32[6,1,2048]{2,1,0:T(1,128)S(1)}, f32[6,1,2048]{2,1,0:T(1,128)S(1)}, u32[]{:S(2)}, u32[]{:S(2)}) collective-permute-start(f32[6,1,2048]{2,1,0:T(1,128)S(1)} %get-tuple-element.585), channel_id=1, source_target_pairs={{1,0},{2,1},{3,2},{0,3},{5,4},{6,5},{7,6},{4,7},{9,8},{10,9},{11,1... | collective-permute-start | bytes 147464 | tf_op jit(solution)/shard_map/ppermute | solution.py:31
  232.8 14.0 %collective-permute-start.9 = (f32[1,8,2048]{2,1,0:T(8,128)S(1)}, f32[1,8,2048]{2,1,0:T(8,128)}, u32[]{:S(2)}, u32[]{:S(2)}) collective-permute-start(f32[1,8,2048]{2,1,0:T(8,128)S(1)} %slice.1185), channel_id=1, source_target_pairs={{4,0},{8,4},{12,8},{16,12},{20,16},{24,20},{28,24},{0,28},{5,1},{9... | collective-permute-start | bytes 196616 | tf_op jit(solution)/shard_map/ppermute | solution.py:31
  235.1 10.9 %collective-permute-start.8 = (f32[1,8,2048]{2,1,0:T(8,128)S(1)}, f32[1,8,2048]{2,1,0:T(8,128)}, u32[]{:S(2)}, u32[]{:S(2)}) collective-permute-start(f32[1,8,2048]{2,1,0:T(8,128)S(1)} %slice.1183), channel_id=1, source_target_pairs={{0,4},{4,8},{8,12},{12,16},{16,20},{20,24},{24,28},{28,0},{1,5},{5... | collective-permute-start | bytes 196616 | tf_op jit(solution)/shard_map/ppermute | solution.py:28
  248.5 9.9 %collective-permute-start.10 = (f32[6,1,2048]{2,1,0:T(1,128)S(1)}, f32[6,1,2048]{2,1,0:T(1,128)S(1)}, u32[]{:S(2)}, u32[]{:S(2)}) collective-permute-start(f32[6,1,2048]{2,1,0:T(1,128)S(1)} %get-tuple-element.582), channel_id=1, source_target_pairs={{0,1},{1,2},{2,3},{3,0},{4,5},{5,6},{6,7},{7,4},{8,9},{9,10},{10,1... | collective-permute-start | bytes 147464 | tf_op jit(solution)/shard_map/ppermute | solution.py:28
  248.5 9.9 %collective-permute-start.11 = (f32[6,1,2048]{2,1,0:T(1,128)S(1)}, f32[6,1,2048]{2,1,0:T(1,128)S(1)}, u32[]{:S(2)}, u32[]{:S(2)}) collective-permute-start(f32[6,1,2048]{2,1,0:T(1,128)S(1)} %get-tuple-element.583), channel_id=1, source_target_pairs={{1,0},{2,1},{3,2},{0,3},{5,4},{6,5},{7,6},{4,7},{9,8},{10,9},{11,1... | collective-permute-start | bytes 147464 | tf_op jit(solution)/shard_map/ppermute | solution.py:31
  273.7 14.1 %collective-permute-start.13 = (f32[1,8,2048]{2,1,0:T(8,128)S(1)}, f32[1,8,2048]{2,1,0:T(8,128)S(1)}, u32[]{:S(2)}, u32[]{:S(2)}) collective-permute-start(f32[1,8,2048]{2,1,0:T(8,128)S(1)} %slice.1209), channel_id=1, source_target_pairs={{4,0},{8,4},{12,8},{16,12},{20,16},{24,20},{28,24},{0,28},{5,1},{9... | collective-permute-start | bytes 196616 | tf_op jit(solution)/shard_map/ppermute | solution.py:31
  276.0 11.7 %collective-permute-start.12 = (f32[1,8,2048]{2,1,0:T(8,128)S(1)}, f32[1,8,2048]{2,1,0:T(8,128)S(1)}, u32[]{:S(2)}, u32[]{:S(2)}) collective-permute-start(f32[1,8,2048]{2,1,0:T(8,128)S(1)} %slice.1207), channel_id=1, source_target_pairs={{0,4},{4,8},{8,12},{12,16},{16,20},{20,24},{24,28},{28,0},{1,5},{5... | collective-permute-start | bytes 196616 | tf_op jit(solution)/shard_map/ppermute | solution.py:28
  288.6 8.7 %collective-permute-start.14 = (f32[6,1,2048]{2,1,0:T(1,128)S(1)}, f32[6,1,2048]{2,1,0:T(1,128)S(1)}, u32[]{:S(2)}, u32[]{:S(2)}) collective-permute-start(f32[6,1,2048]{2,1,0:T(1,128)S(1)} %get-tuple-element.580), channel_id=1, source_target_pairs={{0,1},{1,2},{2,3},{3,0},{4,5},{5,6},{6,7},{7,4},{8,9},{9,10},{10,1... | collective-permute-start | bytes 147464 | tf_op jit(solution)/shard_map/ppermute | solution.py:28
  288.7 8.6 %collective-permute-start.15 = (f32[6,1,2048]{2,1,0:T(1,128)S(1)}, f32[6,1,2048]{2,1,0:T(1,128)S(1)}, u32[]{:S(2)}, u32[]{:S(2)}) collective-permute-start(f32[6,1,2048]{2,1,0:T(1,128)S(1)} %get-tuple-element.581), channel_id=1, source_target_pairs={{1,0},{2,1},{3,2},{0,3},{5,4},{6,5},{7,6},{4,7},{9,8},{10,9},{11,1... | collective-permute-start | bytes 147464 | tf_op jit(solution)/shard_map/ppermute | solution.py:31
  321.6 14.1 %collective-permute-start.17 = (f32[1,8,2048]{2,1,0:T(8,128)S(1)}, f32[1,8,2048]{2,1,0:T(8,128)}, u32[]{:S(2)}, u32[]{:S(2)}) collective-permute-start(f32[1,8,2048]{2,1,0:T(8,128)S(1)} %slice.1233), channel_id=1, source_target_pairs={{4,0},{8,4},{12,8},{16,12},{20,16},{24,20},{28,24},{0,28},{5,1},{9... | collective-permute-start | bytes 196616 | tf_op jit(solution)/shard_map/ppermute | solution.py:31
  324.0 10.9 %collective-permute-start.16 = (f32[1,8,2048]{2,1,0:T(8,128)S(1)}, f32[1,8,2048]{2,1,0:T(8,128)}, u32[]{:S(2)}, u32[]{:S(2)}) collective-permute-start(f32[1,8,2048]{2,1,0:T(8,128)S(1)} %slice.1231), channel_id=1, source_target_pairs={{0,4},{4,8},{8,12},{12,16},{16,20},{20,24},{24,28},{28,0},{1,5},{5... | collective-permute-start | bytes 196616 | tf_op jit(solution)/shard_map/ppermute | solution.py:28
  338.0 8.6 %collective-permute-start.18 = (f32[6,1,2048]{2,1,0:T(1,128)}, f32[6,1,2048]{2,1,0:T(1,128)}, u32[]{:S(2)}, u32[]{:S(2)}) collective-permute-start(f32[6,1,2048]{2,1,0:T(1,128)} %get-tuple-element.578), channel_id=1, source_target_pairs={{0,1},{1,2},{2,3},{3,0},{4,5},{5,6},{6,7},{7,4},{8,9},{9,10},{10,1... | collective-permute-start | bytes 147464 | tf_op jit(solution)/shard_map/ppermute | solution.py:28
  338.0 8.6 %collective-permute-start.19 = (f32[6,1,2048]{2,1,0:T(1,128)}, f32[6,1,2048]{2,1,0:T(1,128)}, u32[]{:S(2)}, u32[]{:S(2)}) collective-permute-start(f32[6,1,2048]{2,1,0:T(1,128)} %get-tuple-element.579), channel_id=1, source_target_pairs={{1,0},{2,1},{3,2},{0,3},{5,4},{6,5},{7,6},{4,7},{9,8},{10,9},{11,1... | collective-permute-start | bytes 147464 | tf_op jit(solution)/shard_map/ppermute | solution.py:31
  (32 other events, 231.9 us)
where the time goes:
time: 359 us; the launch traced here: 353 us
  local copies, waits for them, and re-layouts  109 us (30%)
  other arithmetic  78.8 us (22%)
  matrix products  78.2 us (22%)
  blocking collectives  54.6 us (15%)
  starting transfers between devices  29.6 us (8%)
    psum x1, blocking collectives, shards(): lax.psum((grad_first, grad_second), ('solver', 'group'))  40 us
    ppermute x10, starting transfers between devices, with_halo(): lax.ppermute(lax.slice_in_dim(block, 0, width, axis=dim), axis, backward)  27.6 us
    psum x1, blocking collectives, shards(): counts = lax.psum(jnp.sum(columns, axis=0), 'solver')  14.6 us
    dot_general x5, matrix products, flow_step(): jnp.einsum('ai,ijke->ajke', second_deriv, field, precision=HIGH)  14 us
    dot_general x3, matrix products, network_output(): output = jnp.dot(second_weight.T, mixed, preferred_element_type=jnp.float32)  13.9 us
    mul x5, other arithmetic, flow_step(): change = change.at[:, 0].add(gain * lower_term)  11.9 us
    slice x5, other arithmetic, flow_step(): lower_jump = PENALTY * (upper[..., :-1] - lower[..., 1:])  11.7 us
    dot_general x3, matrix products, network_output(): jnp.einsum('hbn,nm->hbm', hidden.reshape(width, -1, tile), adjacency, pre...  11 us
  transfers between devices with their start and end apart: 20, of which 0 were waited for; matrix products, arithmetic and copies ran while one was open for 47% of the time, Pallas kernels for 0%

commit v1 on v0

v1 whole, which is shorter than its diff:
```python
import jax
import jax.numpy as jnp
import numpy as np
from jax import lax
from jax.experimental import pallas as pl
from jax.experimental.pallas import tpu as pltpu
from jax.sharding import PartitionSpec as P

FLOW_STEPS = 5
EXL = 4
EZL = 8
EY = 8

HIGH = lax.Precision.HIGHEST
TIME_STEP = 0.002
VISCOSITY = 0.01
VELOCITY = 1.0
PENALTY = 1.0
STRESS_SCALE = 0.1
LEARN_RATE = 0.05
LANES = 128
F32 = jnp.float32
BF16 = jnp.bfloat16


def legendre_table(points_x, points):
    table = np.zeros((points_x.shape[0], points))
    table[:, 0] = 1.0
    table[:, 1] = points_x
    for degree in range(2, points):
        table[:, degree] = (
            (2 * degree - 1) * points_x * table[:, degree - 1] - (degree - 1) * table[:, degree - 2]
        ) / degree
    return table


def gll_tables(points):
    order = points - 1
    guess = np.cos(np.pi * np.arange(points) / order)
    for sweep in range(100):
        table = legendre_table(guess, points)
        guess = guess - (guess * table[:, order] - table[:, order - 1]) / (points * table[:, order])
    nodes = guess[::-1]
    values = legendre_table(nodes, points)[:, order]
    matrix = np.zeros((points, points))
    for row in range(points):
        for column in range(points):
            if row != column:
                matrix[row, column] = values[row] / (values[column] * (nodes[row] - nodes[column]))
    matrix[0, 0] = -order * (order + 1) / 4.0
    matrix[order, order] = order * (order + 1) / 4.0
    return matrix.astype(np.float32), 2.0 / (order * (order + 1))


def element_operator(deriv, gain):
    points = deriv.shape[0]
    last = points - 1
    deriv = deriv.astype(np.float64)
    second = 4.0 * VISCOSITY * (deriv @ deriv)
    along_i = -2.0 * VELOCITY * deriv + second
    along_i[0, 0] -= gain * (VELOCITY + PENALTY)
    along_i[last, last] -= gain * PENALTY
    other = second.copy()
    other[0, 0] -= gain * PENALTY
    other[last, last] -= gain * PENALTY
    eye = np.eye(points)
    whole = (
        np.kron(np.kron(along_i, eye), eye)
        + np.kron(np.kron(eye, other), eye)
        + np.kron(np.kron(eye, eye), other)
    )
    whole = (TIME_STEP * whole).astype(np.float32)
    high = whole.astype(jnp.bfloat16)
    low = (whole - high.astype(np.float32)).astype(jnp.bfloat16)
    return high, low


def make_kernel(learners, groups, points, width, deriv, gain):
    face = points * points
    last = points - 1
    nodes = face * points
    walls = EXL * EZL
    elements = walls * EY
    per_tile = LANES // walls
    tiles = face // per_tile
    pairs = tiles // 2
    owners = min(learners, width // LANES)
    owned = width // owners
    devices = learners * groups
    block = EZL * EY
    half = LANES // 2
    step_gain = float(TIME_STEP * gain * PENALTY)
    step_gain_x = float(TIME_STEP * gain * (VELOCITY + PENALTY))
    first_row = [float(value) for value in deriv[0]]

    def roll(value, shift):
        shift = shift % LANES
        return value if shift == 0 else pltpu.roll(value, shift, 1)

    def kernel(
        field_ref, first_ref, second_ref, edges_ref, index_ref, route_ref, high_ref, low_ref,
        out_ref, new_first_ref, new_second_ref,
        u_ref, v_ref, mask_ref, feat_ref, z_ref, grow_ref, w2_ref, acc_ref,
        count_ref, tile_ref, part_ref, cross_ref, total_ref, stress_ref,
        xs_ref, xr_ref, zs_ref, zr_ref,
        count_send, count_recv, part_send, part_recv, cross_send, cross_recv,
        total_send, total_recv, xs_send, xr_recv, zs_send, zr_recv,
    ):
        me = lax.axis_index("solver")
        mine = lax.axis_index("group")

        def peer_s(offset):
            return lax.rem(me + offset, learners)

        def peer_g(offset):
            return lax.rem(mine + offset, groups)

        barrier = pltpu.get_barrier_semaphore()
        for offset in range(1, learners):
            pl.semaphore_signal(
                barrier, inc=1, device_id={"solver": peer_s(offset)},
                device_id_type=pl.DeviceIdType.MESH,
            )
        for offset in range(1, groups):
            pl.semaphore_signal(
                barrier, inc=1, device_id={"group": peer_g(offset)},
                device_id_type=pl.DeviceIdType.MESH,
            )

        def remote(source, target, send, recv, where):
            return pltpu.make_async_remote_copy(
                src_ref=source, dst_ref=target, send_sem=send, recv_sem=recv,
                device_id=where, device_id_type=pl.DeviceIdType.MESH,
            )

        lane = lax.broadcasted_iota(jnp.int32, (1, LANES), 1)
        low_half = lane < half
        slot = lax.rem(lane, block) // EY
        level = lax.rem(lane, EY)

        learner_rows = lax.broadcasted_iota(jnp.int32, (learners, route_ref.shape[1]), 0)
        hits = (route_ref[...] == learner_rows).astype(F32)
        count_ref[me] = jnp.broadcast_to(jnp.sum(hits, axis=1, keepdims=True), (learners, LANES))

        def copies(step):
            right, left = {"solver": peer_s(1)}, {"solver": peer_s(learners - 1)}
            up, down = {"group": peer_g(1)}, {"group": peer_g(groups - 1)}
            result = []
            for side, where in ((0, right), (1, left)):
                result.append(remote(
                    xs_ref.at[step, side], xr_ref.at[step, side],
                    xs_send.at[step, side], xr_recv.at[step, side], where))
            for side, where in ((0, up), (1, down)):
                result.append(remote(
                    zs_ref.at[step, side], zr_ref.at[step, side],
                    zs_send.at[step, side], zr_recv.at[step, side], where))
            return result

        half_face = face // 2

        def send_faces(step):
            upper = u_ref[1, pl.ds(nodes - face, face), :]
            xs_ref[step, 0] = jnp.where(low_half, roll(upper[:half_face], half), upper[half_face:])
            lower = u_ref[0, pl.ds(0, face), :]
            xs_ref[step, 1] = jnp.where(low_half, lower[:half_face], roll(lower[half_face:], half))
            for part in range(2):
                high_pack = jnp.zeros((points, LANES), F32)
                low_pack = jnp.zeros((points, LANES), F32)
                for i in range(points):
                    top = u_ref[part, pl.ds(i * face + last, points, stride=points), :]
                    high_pack = jnp.where(slot == i, roll(top, EY * (i + 1)), high_pack)
                    bottom = u_ref[part, pl.ds(i * face, points, stride=points), :]
                    low_pack = jnp.where(slot == i, roll(bottom, EY * i), low_pack)
                zs_ref[step, 0, part] = high_pack
                zs_ref[step, 1, part] = low_pack
            for copy in copies(step):
                copy.start()

        for part in range(2):
            u_ref[part] = field_ref[:, part * LANES:(part + 1) * LANES]
        pl.semaphore_wait(barrier, learners + groups - 2)
        for offset in range(1, learners):
            remote(count_ref.at[me], count_ref.at[me], count_send.at[offset], count_recv.at[me],
                   {"solver": peer_s(offset)}).start()
        send_faces(0)

        rows = lax.broadcasted_iota(jnp.int32, (elements, LANES), 0)
        cols = lax.broadcasted_iota(jnp.int32, (elements, LANES), 1)
        picked = jnp.zeros((tiles * points, LANES), F32)
        first_select = None
        for q in range(per_tile):
            local = cols - q * walls
            select = ((rows == local * EY) & (local >= 0) & (local < walls)).astype(F32).astype(BF16)
            if q == 0:
                first_select = select
            pieces = []
            for m in range(tiles):
                node = m * per_tile + q
                start = (node // points) * face + node % points
                pieces.append(jnp.concatenate(
                    [u_ref[part, pl.ds(start, points, stride=points), :] for part in range(2)],
                    axis=1))
            stacked = jnp.concatenate(pieces, axis=0).astype(BF16)
            picked = picked + jnp.dot(stacked, select, preferred_element_type=F32)
        for m in range(tiles):
            feat_ref[m // 2, :, pl.ds((m % 2) * LANES, LANES)] = picked[m * points:(m + 1) * points]
        slopes = []
        for i in range(points):
            total = None
            for j in range(points):
                term = first_row[j] * field_ref[pl.ds(i * face + j * points, points), :]
                total = term if total is None else total + term
            slopes.append(STRESS_SCALE * total)
        target = jnp.dot(
            jnp.concatenate(slopes, axis=0).astype(BF16), first_select, preferred_element_type=F32
        )

        edge_rows = lax.broadcasted_iota(jnp.int32, (face, edges_ref.shape[1]), 0)
        tile_rows = lax.rem(edge_rows, tiles) * per_tile + edge_rows // tiles
        source = (edges_ref[0:1, :] == tile_rows).astype(F32).astype(BF16)
        sink = (edges_ref[1:2, :] == edge_rows).astype(F32).astype(BF16)
        contract = (((1,), (1,)), ((), ()))
        node_rows = lax.broadcasted_iota(jnp.int32, (face, face), 0)
        node_cols = lax.broadcasted_iota(jnp.int32, (face, face), 1)
        tile_node_rows = lax.rem(node_rows, tiles) * per_tile + node_rows // tiles
        tile_node_cols = lax.rem(node_cols, tiles) * per_tile + node_cols // tiles
        backward = 0.25 * lax.dot_general(source, sink, contract, preferred_element_type=F32)
        backward = backward + (tile_node_rows == node_cols).astype(F32)
        forward = 0.25 * lax.dot_general(sink, source, contract, preferred_element_type=F32)
        forward = forward + (node_rows == tile_node_cols).astype(F32)

        def network(first, second, keep_mask):
            turned = jnp.transpose(first).astype(BF16)
            w2_ref[...] = jnp.transpose(jnp.broadcast_to(second, (LANES, width)))

            def one(pair, carry):
                before = jnp.dot(turned, feat_ref[pair].astype(BF16), preferred_element_type=F32)
                if keep_mask:
                    mask_ref[pair] = jnp.where(before > 0.0, 1.0, 0.0).astype(BF16)
                hidden = jnp.maximum(before, 0.0)
                weight = w2_ref[...]
                z_ref[pl.ds(2 * pair, 1), :] = jnp.sum(
                    hidden[:, :LANES] * weight, axis=0, keepdims=True)
                z_ref[pl.ds(2 * pair + 1, 1), :] = jnp.sum(
                    hidden[:, LANES:] * weight, axis=0, keepdims=True)
                return carry

            lax.fori_loop(0, pairs, one, 0)
            z = z_ref[...]
            stacked = jnp.concatenate([roll(z, -walls * q) for q in range(per_tile)], axis=0)
            return jnp.dot(forward, stacked, precision=HIGH, preferred_element_type=F32)

        first = first_ref[...].astype(F32)
        second = second_ref[...].astype(F32)
        output = network(first, second, True)

        for offset in range(1, learners):
            origin = peer_s(offset)
            remote(count_ref.at[me], count_ref.at[origin], count_send.at[offset],
                   count_recv.at[origin], {"solver": origin}).wait_recv()
        counts = count_ref[0]
        for other in range(1, learners):
            counts = counts + count_ref[other]
        inverse = 1.0 / (jnp.maximum(counts[:, 0:1], 1.0) * devices)
        share = jnp.sum(hits * inverse, axis=0, keepdims=True)
        places = lax.broadcasted_iota(jnp.int32, (LANES, index_ref.shape[1]), 0)
        chosen = (index_ref[...] == places).astype(F32)
        weight = lax.dot_general(
            jnp.broadcast_to(share, (8, share.shape[1])), chosen, contract,
            precision=HIGH, preferred_element_type=F32,
        )[0:1]

        error = ((output - target) * weight).astype(BF16).astype(F32)
        g = jnp.dot(backward, error, precision=HIGH, preferred_element_type=F32)
        spread = g[0:tiles]
        for q in range(1, per_tile):
            spread = spread + roll(g[q * tiles:(q + 1) * tiles], walls * q)
        grow_ref[...] = spread
        acc_ref[...] = jnp.zeros_like(acc_ref)

        def back(pair, carry):
            scale = jnp.concatenate(
                [grow_ref[pl.ds(2 * pair, 1), :], grow_ref[pl.ds(2 * pair + 1, 1), :]], axis=1)
            scaled = feat_ref[pair] * scale
            upper = scaled.astype(BF16).astype(F32)
            both = jnp.concatenate([upper, scaled - upper], axis=0).astype(BF16)
            acc_ref[...] += lax.dot_general(
                both, mask_ref[pair], contract, preferred_element_type=F32)
            return carry

        lax.fori_loop(0, pairs, back, 0)
        grad = acc_ref[0:points, :] + acc_ref[points:2 * points, :]
        for t in range(owners):
            tile_ref[t] = grad[:, t * owned:(t + 1) * owned]

        def when_owner(which, action):
            if owners == learners:
                action()
            else:
                pl.when(which < owners)(action)

        def part_copy(offset):
            where = peer_s(offset)
            at = where if owners == learners else jnp.minimum(where, owners - 1)
            return where, remote(tile_ref.at[at], part_ref.at[me], part_send.at[offset],
                                 part_recv.at[me], {"solver": where})

        for offset in range(1, learners):
            where, copy = part_copy(offset)
            when_owner(where, copy.start)

        def reduce_owned():
            total = tile_ref[me if owners == learners else jnp.minimum(me, owners - 1)]
            for offset in range(1, learners):
                origin = peer_s(offset)
                remote(tile_ref.at[0], part_ref.at[origin], part_send.at[offset],
                       part_recv.at[origin], {"solver": origin}).wait_recv()
            for offset in range(1, learners):
                total = total + part_ref[peer_s(offset)]
            cross_ref[mine] = total
            for offset in range(1, groups):
                remote(cross_ref.at[mine], cross_ref.at[mine], cross_send.at[offset],
                       cross_recv.at[mine], {"group": peer_g(offset)}).start()
            for offset in range(1, groups):
                origin = peer_g(offset)
                remote(cross_ref.at[mine], cross_ref.at[origin], cross_send.at[offset],
                       cross_recv.at[origin], {"group": origin}).wait_recv()
            total = cross_ref[0]
            for other in range(1, groups):
                total = total + cross_ref[other]
            total_ref[me if owners == learners else jnp.minimum(me, owners - 1)] = total
            at = me if owners == learners else jnp.minimum(me, owners - 1)
            for offset in range(1, learners):
                remote(total_ref.at[at], total_ref.at[at], total_send.at[offset],
                       total_recv.at[at], {"solver": peer_s(offset)}).start()

        when_owner(me, reduce_owned)
        for offset in range(1, learners):
            origin = peer_s(offset)
            at = origin if owners == learners else jnp.minimum(origin, owners - 1)
            copy = remote(total_ref.at[at], total_ref.at[at], total_send.at[offset],
                          total_recv.at[at], {"solver": origin})
            when_owner(origin, copy.wait_recv)

        grad = jnp.concatenate([total_ref[t] for t in range(owners)], axis=1)
        new_first = (first - LEARN_RATE * (grad * second)).astype(BF16)
        grad_second = jnp.sum(first * grad, axis=0, keepdims=True)
        new_second = (second - LEARN_RATE * grad_second).astype(BF16)
        new_first_ref[...] = new_first
        new_second_ref[...] = new_second

        output = network(new_first.astype(F32), new_second.astype(F32), False)
        rows_t = lax.broadcasted_iota(jnp.int32, (LANES, elements), 0)
        cols_t = lax.broadcasted_iota(jnp.int32, (LANES, elements), 1)
        place = ((cols_t == rows_t * EY) & (rows_t < walls)).astype(F32)
        stress_ref[...] = jnp.dot(output, place, precision=HIGH, preferred_element_type=F32)

        def flow(step, carry):
            u = jnp.concatenate([u_ref[0], u_ref[1]], axis=1)
            upper = u.astype(BF16)
            lower = (u - upper.astype(F32)).astype(BF16)
            change = (
                jnp.dot(high_ref[...], upper, preferred_element_type=F32)
                + jnp.dot(high_ref[...], lower, preferred_element_type=F32)
                + jnp.dot(low_ref[...], upper, preferred_element_type=F32)
            )
            u = u + change
            for part in range(2):
                v_ref[part] = u[:, part * LANES:(part + 1) * LANES]
            for part in range(2):
                columns = pl.ds(part * LANES, LANES)
                for i in range(points):
                    base = i * face
                    bottom = u_ref[part, pl.ds(base, points), :]
                    top = u_ref[part, pl.ds(base + face - points, points), :]
                    stress = stress_ref[pl.ds(i * points, points), columns]
                    below = jnp.where(level == 0, bottom + stress, roll(top, 1))
                    above = jnp.where(level == EY - 1, 0.0, roll(bottom, -1))
                    v_ref[part, pl.ds(base, points), :] += step_gain * below
                    v_ref[part, pl.ds(base + face - points, points), :] += step_gain * above
            for copy in copies(step):
                copy.wait_recv()
            low0 = roll(u_ref[0, pl.ds(nodes - face, face), :], half)
            low1 = roll(u_ref[1, pl.ds(nodes - face, face), :], half)
            halo = xr_ref[step, 0]
            halo = jnp.concatenate([halo, roll(halo, half)], axis=0)
            v_ref[0, pl.ds(0, face), :] += step_gain_x * jnp.where(low_half, halo, low0)
            v_ref[1, pl.ds(0, face), :] += step_gain_x * jnp.where(low_half, low0, low1)
            high0 = roll(u_ref[0, pl.ds(0, face), :], half)
            high1 = roll(u_ref[1, pl.ds(0, face), :], half)
            halo = xr_ref[step, 1]
            halo = jnp.concatenate([roll(halo, half), halo], axis=0)
            v_ref[0, pl.ds(nodes - face, face), :] += step_gain * jnp.where(
                low_half, high0, high1)
            v_ref[1, pl.ds(nodes - face, face), :] += step_gain * jnp.where(
                low_half, high1, halo)
            for part in range(2):
                before_pack = zr_ref[step, 0, part]
                after_pack = zr_ref[step, 1, part]
                for i in range(points):
                    near = pl.ds(i * face, points, stride=points)
                    far = pl.ds(i * face + last, points, stride=points)
                    top = u_ref[part, far, :]
                    bottom = u_ref[part, near, :]
                    before = jnp.where(slot == 0, roll(before_pack, half - EY * i), roll(top, EY))
                    after = jnp.where(
                        slot == EZL - 1, roll(after_pack, EY * (EZL - 1 - i)), roll(bottom, -EY))
                    v_ref[part, near, :] = v_ref[part, near, :] + step_gain * before
                    v_ref[part, far, :] = v_ref[part, far, :] + step_gain * after
            u_ref[...] = v_ref[...]

            @pl.when(step < FLOW_STEPS - 1)
            def _():
                send_faces(step + 1)

            return carry

        lax.fori_loop(0, FLOW_STEPS, flow, 0)
        for part in range(2):
            out_ref[:, part * LANES:(part + 1) * LANES] = v_ref[part]

        for offset in range(1, learners):
            remote(count_ref.at[me], count_ref.at[me], count_send.at[offset], count_recv.at[me],
                   {"solver": peer_s(offset)}).wait_send()
            where, copy = part_copy(offset)
            when_owner(where, copy.wait_send)

        def drain_owned():
            at = me if owners == learners else jnp.minimum(me, owners - 1)
            for offset in range(1, groups):
                remote(cross_ref.at[mine], cross_ref.at[mine], cross_send.at[offset],
                       cross_recv.at[mine], {"group": peer_g(offset)}).wait_send()
            for offset in range(1, learners):
                remote(total_ref.at[at], total_ref.at[at], total_send.at[offset],
                       total_recv.at[at], {"solver": peer_s(offset)}).wait_send()

        when_owner(me, drain_owned)

        def drain(step, carry):
            for copy in copies(step):
                copy.wait_send()
            return carry

        lax.fori_loop(0, FLOW_STEPS, drain, 0)

    dma = pltpu.SemaphoreType.DMA
    scratch = [
        pltpu.VMEM((2, nodes, LANES), F32),
        pltpu.VMEM((2, nodes, LANES), F32),
        pltpu.VMEM((pairs, width, 2 * LANES), BF16),
        pltpu.VMEM((pairs, points, 2 * LANES), F32),
        pltpu.VMEM((tiles, LANES), F32),
        pltpu.VMEM((tiles, LANES), F32),
        pltpu.VMEM((width, LANES), F32),
        pltpu.VMEM((2 * points, width), F32),
        pltpu.VMEM((learners, learners, LANES), F32),
        pltpu.VMEM((owners, points, owned), F32),
        pltpu.VMEM((learners, points, owned), F32),
        pltpu.VMEM((groups, points, owned), F32),
        pltpu.VMEM((owners, points, owned), F32),
        pltpu.VMEM((face, elements), F32),
        pltpu.VMEM((FLOW_STEPS, 2, face // 2, LANES), F32),
        pltpu.VMEM((FLOW_STEPS, 2, face // 2, LANES), F32),
        pltpu.VMEM((FLOW_STEPS, 2, 2, points, LANES), F32),
        pltpu.VMEM((FLOW_STEPS, 2, 2, points, LANES), F32),
        dma((learners,)), dma((learners,)), dma((learners,)), dma((learners,)),
        dma((groups,)), dma((groups,)), dma((learners,)), dma((owners,)),
        dma((FLOW_STEPS, 2)), dma((FLOW_STEPS, 2)), dma((FLOW_STEPS, 2)), dma((FLOW_STEPS, 2)),
    ]
    return kernel, scratch


def shards(field, first_weight, second_weight, face_edges, sample_index, route):
    points = field.shape[0]
    elements = field.shape[3]
    nodes = points**3
    width = first_weight.shape[1]
    learners = lax.axis_size("solver")
    groups = lax.axis_size("group")
    deriv, end_weight = gll_tables(points)
    gain = 2.0 / end_weight
    high, low = element_operator(deriv, gain)
    kernel, scratch = make_kernel(learners, groups, points, width, deriv, gain)
    vmem = pl.BlockSpec(memory_space=pltpu.VMEM)
    new_field, new_first, new_second = pl.pallas_call(
        kernel,
        out_shape=(
            jax.ShapeDtypeStruct((nodes, elements), F32),
            jax.ShapeDtypeStruct(first_weight.shape, BF16),
            jax.ShapeDtypeStruct((1, width), BF16),
        ),
        in_specs=[vmem] * 8,
        out_specs=(vmem, vmem, vmem),
        scratch_shapes=scratch,
        compiler_params=pltpu.CompilerParams(
            collective_id=0, has_side_effects=True, vmem_limit_bytes=40 * 1024 * 1024
        ),
        name="step",
    )(
        field.reshape(nodes, elements),
        first_weight,
        second_weight.reshape(1, width),
        face_edges,
        sample_index.reshape(1, -1),
        route.reshape(1, -1),
        jnp.asarray(high),
        jnp.asarray(low),
    )
    return (new_field.reshape(field.shape), new_first, new_second.reshape(second_weight.shape))


def solution(mesh):
    return jax.shard_map(
        shards,
        mesh=mesh,
        in_specs=(
            P(None, None, None, ("solver", "group")),
            P(),
            P(),
            P(),
            P(("solver", "group")),
            P(("solver", "group"), None),
        ),
        out_specs=(P(None, None, None, ("solver", "group")), P(), P()),
        check_vma=False,
    )
```

time: 359 us -> 49.7 us (0.14); the launches traced: 353 us -> 49.4 us
  local copies, waits for them, and re-layouts: 109 us -> 6.5 us
  other arithmetic: 78.8 us -> 0 us
  matrix products: 78.2 us -> 0 us
  blocking collectives: 54.6 us -> 0 us
  Pallas kernels: 0 us -> 42.2 us
  starting transfers between devices: 29.6 us -> 0 us
    dot_general x39 -> x0, matrix products: 78.2 us -> none  [the longest x5 14 us: flow_step(): jnp.einsum('ai,ijke->ajke', second_deriv, field, precision=HIGH)]
    psum x2 -> x0, blocking collectives: 54.6 us -> none  [the longest x1 40 us: shards(): lax.psum((grad_first, grad_second), ('solver', 'group'))]
    pallas_call x0 -> x1, Pallas kernels: none -> 42.2 us  [shards(): pl.pallas_call(kernel, out_shape=(jax.ShapeDtypeStruct((nodes, elements),...]
    ppermute x20 -> x0, starting transfers between devices: 29.6 us -> none  [the longest x10 27.6 us: with_halo(): lax.ppermute(lax.slice_in_dim(block, 0, width, axis=dim), axis, backward)]
    slice x90 -> x0, local copies, waits for them, and re-layouts: 19 us -> none  [the longest x10 7.17 us: neighbour_faces(): after_z = unpack(padded[1:EXL + 1, 2:, :, 2])]
    mul x9 -> x0, other arithmetic: 16.8 us -> none  [the longest x5 11.9 us: flow_step(): change = change.at[:, 0].add(gain * lower_term)]
    scatter-add x20 -> x0, other arithmetic: 15.8 us -> none  [the longest x5 3.97 us: flow_step(): change.at[:, :, 0].add(gain * PENALTY * (before_z - field[:, :, 0]))]
    convert_element_type x15 -> x0, other arithmetic: 15.4 us -> none  [the longest x2 9.95 us: network_output(): mixed = (hidden.astype(jnp.float32) + spread).astype(jnp.bfloat16)]
  transfers between devices with their start and end apart: 20 -> 0, of which waited for: 0 -> 0; matrix products, arithmetic and copies ran while one was open for 47% -> 0% of each run, Pallas kernels for 0% -> 0%
where the time goes in v1:
time: 49.7 us; the launch traced here: 49.4 us
  Pallas kernels  42.2 us (85%)
  local copies, waits for them, and re-layouts  6.5 us (13%)
  between operations  0.68 us (1%)
    pallas_call x1, Pallas kernels, shards(): pl.pallas_call(kernel, out_shape=(jax.ShapeDtypeStruct((nodes, elements),...  42.2 us
    unnamed x19, local copies, waits for them, and re-layouts  6.5 us

profile of v1, /device:TPU:0, one launch (start us, length us, event | category | flops | bytes accessed | tf_op | source)
XLA Modules:
  0.0 49.4 jit_solution(13651340189640940288)
XLA Ops:
  0.6 0.0 copy-start.4
  0.6 0.0 copy-start.5
  0.7 0.0 copy-start.6
  0.7 0.0 copy-start.7
  0.7 0.6 %copy-done.4 = bf16[1024,1]{0,1:T(2,128)(2,1)S(1)} copy-done((bf16[1024,1]{0,1:T(2,128)(2,1)S(1)}, bf16[1024,1]{0,1:T(2,128)(2,1)}, u32[]{:S(2)}) %copy-start.4) | copy-done | bytes 2072
  1.3 0.0 copy-done.5
  1.3 0.0 copy-done.6
  1.3 0.0 copy-done.7
  1.3 0.0 copy-start
  1.3 1.0 %copy-done = f32[8,8,8,256]{3,2,1,0:T(8,128)S(1)} copy-done((f32[8,8,8,256]{3,2,1,0:T(8,128)S(1)}, f32[8,8,8,256]{3,2,1,0:T(8,128)}, u32[]{:S(2)}) %copy-start) | copy-done | bytes 524312
  2.4 0.0 copy-start.1
  2.4 1.0 %copy-done.1 = bf16[512,512]{1,0:T(8,128)(2,1)S(1)} copy-done((bf16[512,512]{1,0:T(8,128)(2,1)S(1)}, bf16[512,512]{1,0:T(8,128)(2,1)}, u32[]{:S(2)}) %copy-start.1) | copy-done | bytes 524312
  3.4 0.0 copy-start.2
  3.4 1.0 %copy-done.2 = bf16[512,512]{1,0:T(8,128)(2,1)S(1)} copy-done((bf16[512,512]{1,0:T(8,128)(2,1)S(1)}, bf16[512,512]{1,0:T(8,128)(2,1)}, u32[]{:S(2)}) %copy-start.2) | copy-done | bytes 524312
  4.5 0.0 copy-start.3
  4.5 0.7 %copy-done.3 = bf16[8,1024]{1,0:T(8,128)(2,1)S(1)} copy-done((bf16[8,1024]{1,0:T(8,128)(2,1)S(1)}, bf16[8,1024]{1,0:T(8,128)(2,1)}, u32[]{:S(2)}) %copy-start.3) | copy-done | bytes 16408
  5.2 42.2 %step.1 = (f32[512,256]{1,0:T(8,128)S(1)}, bf16[8,1024]{1,0:T(8,128)(2,1)S(1)}, bf16[1,1024]{1,0:T(2,128)(2,1)S(1)}) custom-call(f32[512,256]{1,0:T(8,128)S(1)} %bitcast.6, bf16[8,1024]{1,0:T(8,128)(2,1)S(1)} %copy-done.3, bf16[1,1024]{1,0:T(2,128)(2,1)S(1)} %bitcast.8, s32[2,256]{1,0:T(2,128)S(1)} %copy-done.5, s32[1,64]{1,0:T(1,128)S(1)} %bitcast.10, ...), custom_call_target="tpu_custom_call" | custom-call | tf_op jit(solution)/shard_map/step/pallas_call | solution.py:485
  47.4 0.8 %copy.14 = f32[8,8,8,256]{3,2,1,0:T(8,128)} copy(f32[8,8,8,256]{3,2,1,0:T(8,128)S(1)} %bitcast.7) | data formatting | bytes 1048576
  48.2 0.6 %copy.15 = bf16[8,1024]{1,0:T(8,128)(2,1)} copy(bf16[8,1024]{1,0:T(8,128)(2,1)S(1)} %get-tuple-element.13) | data formatting | bytes 32768
  48.8 0.6 %copy.16 = bf16[1024,1]{0,1:T(2,128)(2,1)} copy(bf16[1024,1]{0,1:T(2,128)(2,1)S(1)} %bitcast.9) | data formatting | bytes 4096
Async XLA Ops:
  0.6 0.7 %copy-start.4 = (bf16[1024,1]{0,1:T(2,128)(2,1)S(1)}, bf16[1024,1]{0,1:T(2,128)(2,1)}, u32[]{:S(2)}) copy-start(bf16[1024,1]{0,1:T(2,128)(2,1)} %param.10) | copy-start | bytes 6148
  0.6 0.7 %copy-start.5 = (s32[2,256]{1,0:T(2,128)S(1)}, s32[2,256]{1,0:T(2,128)}, u32[]{:S(2)}) copy-start(s32[2,256]{1,0:T(2,128)} %edges_ref.1) | copy-start | bytes 6148
  0.7 0.7 %copy-start.6 = (s32[64]{0:T(128)S(1)}, s32[64]{0:T(128)}, u32[]{:S(2)}) copy-start(s32[64]{0:T(128)} %param.12) | copy-start | bytes 772
  0.7 0.7 %copy-start.7 = (s32[64,1]{0,1:T(1,128)S(1)}, s32[64,1]{0,1:T(1,128)}, u32[]{:S(2)}) copy-start(s32[64,1]{0,1:T(1,128)} %param.13) | copy-start | bytes 772
  1.3 1.0 %copy-start = (f32[8,8,8,256]{3,2,1,0:T(8,128)S(1)}, f32[8,8,8,256]{3,2,1,0:T(8,128)}, u32[]{:S(2)}) copy-start(f32[8,8,8,256]{3,2,1,0:T(8,128)} %param.8) | copy-start | bytes 1572868
  2.4 1.0 %copy-start.1 = (bf16[512,512]{1,0:T(8,128)(2,1)S(1)}, bf16[512,512]{1,0:T(8,128)(2,1)}, u32[]{:S(2)}) copy-start(bf16[512,512]{1,0:T(8,128)(2,1)} %constant.5.clone.low_ref) | copy-start | bytes 1572868
  3.4 1.0 %copy-start.2 = (bf16[512,512]{1,0:T(8,128)(2,1)S(1)}, bf16[512,512]{1,0:T(8,128)(2,1)}, u32[]{:S(2)}) copy-start(bf16[512,512]{1,0:T(8,128)(2,1)} %constant.4.clone.high_ref) | copy-start | bytes 1572868
  4.5 0.7 %copy-start.3 = (bf16[8,1024]{1,0:T(8,128)(2,1)S(1)}, bf16[8,1024]{1,0:T(8,128)(2,1)}, u32[]{:S(2)}) copy-start(bf16[8,1024]{1,0:T(8,128)(2,1)} %first_ref.1) | copy-start | bytes 49156

commit v2 on v1

v2 whole, which is shorter than its diff:
```python
import jax
import jax.numpy as jnp
import numpy as np
from jax import lax
from jax.experimental import pallas as pl
from jax.experimental.pallas import tpu as pltpu
from jax.sharding import PartitionSpec as P

FLOW_STEPS = 5
EXL = 4
EZL = 8
EY = 8

HIGH = lax.Precision.HIGHEST
TIME_STEP = 0.002
VISCOSITY = 0.01
VELOCITY = 1.0
PENALTY = 1.0
STRESS_SCALE = 0.1
LEARN_RATE = 0.05
LANES = 128
F32 = jnp.float32
BF16 = jnp.bfloat16


def legendre_table(points_x, points):
    table = np.zeros((points_x.shape[0], points))
    table[:, 0] = 1.0
    table[:, 1] = points_x
    for degree in range(2, points):
        table[:, degree] = (
            (2 * degree - 1) * points_x * table[:, degree - 1] - (degree - 1) * table[:, degree - 2]
        ) / degree
    return table


def gll_tables(points):
    order = points - 1
    guess = np.cos(np.pi * np.arange(points) / order)
    for sweep in range(100):
        table = legendre_table(guess, points)
        guess = guess - (guess * table[:, order] - table[:, order - 1]) / (points * table[:, order])
    nodes = guess[::-1]
    values = legendre_table(nodes, points)[:, order]
    matrix = np.zeros((points, points))
    for row in range(points):
        for column in range(points):
            if row != column:
                matrix[row, column] = values[row] / (values[column] * (nodes[row] - nodes[column]))
    matrix[0, 0] = -order * (order + 1) / 4.0
    matrix[order, order] = order * (order + 1) / 4.0
    return matrix.astype(np.float32), 2.0 / (order * (order + 1))


def element_operator(deriv, gain):
    points = deriv.shape[0]
    last = points - 1
    deriv = deriv.astype(np.float64)
    second = 4.0 * VISCOSITY * (deriv @ deriv)
    along_i = -2.0 * VELOCITY * deriv + second
    along_i[0, 0] -= gain * (VELOCITY + PENALTY)
    along_i[last, last] -= gain * PENALTY
    other = second.copy()
    other[0, 0] -= gain * PENALTY
    other[last, last] -= gain * PENALTY
    eye = np.eye(points)
    whole = (
        np.kron(np.kron(along_i, eye), eye)
        + np.kron(np.kron(eye, other), eye)
        + np.kron(np.kron(eye, eye), other)
    )
    whole = (TIME_STEP * whole).astype(np.float32)
    high = whole.astype(jnp.bfloat16)
    low = (whole - high.astype(np.float32)).astype(jnp.bfloat16)
    return high, low


def make_kernel(learners, groups, points, width, deriv, gain):
    face = points * points
    last = points - 1
    nodes = face * points
    walls = EXL * EZL
    elements = walls * EY
    pairs = walls * face // (2 * LANES)
    owners = min(learners, width // LANES)
    owned = width // owners
    devices = learners * groups
    block = EZL * EY
    half = LANES // 2
    step_gain = float(TIME_STEP * gain * PENALTY)
    step_gain_x = float(TIME_STEP * gain * (VELOCITY + PENALTY))
    first_row = [float(value) for value in deriv[0]]

    def roll(value, shift):
        shift = shift % LANES
        return value if shift == 0 else pltpu.roll(value, shift, 1)

    rows_sent = points + 1
    lane_rows = walls * face // LANES

    def kernel(
        field_ref, first_ref, second_ref, edges_ref, index_ref, route_ref, high_hbm, low_hbm,
        out_ref, new_first_ref, new_second_ref,
        u_ref, high_ref, low_ref, mask_ref, mixed_ref, feat_ref, turn_ref, z_ref, g_ref, e_ref,
        w2_ref, acc_ref, acc2_ref,
        count_ref, tile_ref, part_ref, cross_ref, total_ref, stress_ref,
        xs_ref, xr_ref, zs_ref, zr_ref,
        load_sem, count_send, count_recv, part_send, part_recv, cross_send, cross_recv,
        total_send, total_recv, xs_send, xr_recv, zs_send, zr_recv,
    ):
        me = lax.axis_index("solver")
        mine = lax.axis_index("group")

        def peer_s(offset):
            return lax.rem(me + offset, learners)

        def peer_g(offset):
            return lax.rem(mine + offset, groups)

        loads = [
            pltpu.make_async_copy(
                field_ref.at[:, pl.ds(part * LANES, LANES)], u_ref.at[0, part], load_sem.at[part])
            for part in range(2)
        ]
        loads.append(pltpu.make_async_copy(high_hbm, high_ref, load_sem.at[2]))
        loads.append(pltpu.make_async_copy(low_hbm, low_ref, load_sem.at[3]))
        for load in loads:
            load.start()

        barrier = pltpu.get_barrier_semaphore()
        for offset in range(1, learners):
            pl.semaphore_signal(
                barrier, inc=1, device_id={"solver": peer_s(offset)},
                device_id_type=pl.DeviceIdType.MESH,
            )
        for offset in range(1, groups):
            pl.semaphore_signal(
                barrier, inc=1, device_id={"group": peer_g(offset)},
                device_id_type=pl.DeviceIdType.MESH,
            )

        def remote(source, target, send, recv, where):
            return pltpu.make_async_remote_copy(
                src_ref=source, dst_ref=target, send_sem=send, recv_sem=recv,
                device_id=where, device_id_type=pl.DeviceIdType.MESH,
            )

        lane = lax.broadcasted_iota(jnp.int32, (1, LANES), 1)
        low_half = lane < half
        slot = lax.rem(lane, block) // EY
        level = lax.rem(lane, EY)
        contract = (((1,), (1,)), ((), ()))

        learner_rows = lax.broadcasted_iota(jnp.int32, (learners, route_ref.shape[1]), 0)
        hits = (route_ref[...] == learner_rows).astype(F32)
        count_ref[me] = jnp.broadcast_to(jnp.sum(hits, axis=1, keepdims=True), (learners, LANES))

        big = 2 * LANES
        edge_rows = lax.rem(
            lax.broadcasted_iota(jnp.int32, (big, edges_ref.shape[1]), 0), face)
        source = (edges_ref[0:1, :] == edge_rows).astype(F32).astype(BF16)
        sink = (edges_ref[1:2, :] == edge_rows).astype(F32).astype(BF16)
        node_rows = lax.broadcasted_iota(jnp.int32, (big, big), 0)
        node_cols = lax.broadcasted_iota(jnp.int32, (big, big), 1)
        graph = 0.25 * lax.dot_general(source, sink, contract, preferred_element_type=F32)
        graph = jnp.where(node_rows // face == node_cols // face, graph, 0.0)
        graph = graph + (node_rows == node_cols).astype(F32)
        small = graph[:LANES, :LANES]
        graph = graph.astype(BF16)
        first = first_ref[...].astype(F32)
        second = second_ref[...].astype(F32)

        def copies(step):
            right, left = {"solver": peer_s(1)}, {"solver": peer_s(learners - 1)}
            up, down = {"group": peer_g(1)}, {"group": peer_g(groups - 1)}
            result = []
            for side, where in ((0, right), (1, left)):
                result.append(remote(
                    xs_ref.at[step, side], xr_ref.at[step, side],
                    xs_send.at[step, side], xr_recv.at[step, side], where))
            for side, where in ((0, up), (1, down)):
                result.append(remote(
                    zs_ref.at[step, side], zr_ref.at[step, side],
                    zs_send.at[step, side], zr_recv.at[step, side], where))
            return result

        half_face = face // 2

        def near(i):
            return pl.ds(i * face, points, stride=points)

        def far(i):
            return pl.ds(i * face + last, points, stride=points)

        def send_z(step, bottoms, tops):
            for part in range(2):
                high_pack = jnp.zeros((points, LANES), F32)
                low_pack = jnp.zeros((points, LANES), F32)
                for i in range(points):
                    high_pack = jnp.where(slot == i, roll(tops[part][i], EY * (i + 1)), high_pack)
                    low_pack = jnp.where(slot == i, roll(bottoms[part][i], EY * i), low_pack)
                zs_ref[step, 0, part] = high_pack
                zs_ref[step, 1, part] = low_pack
            every = copies(step)
            every[2].start()
            every[3].start()

        def send_x(step, u):
            upper = u[1, pl.ds(nodes - face, face), :]
            xs_ref[step, 0] = jnp.where(low_half, roll(upper[:half_face], half), upper[half_face:])
            lower = u[0, pl.ds(0, face), :]
            xs_ref[step, 1] = jnp.where(low_half, lower[:half_face], roll(lower[half_face:], half))
            every = copies(step)
            every[0].start()
            every[1].start()

        def send_faces(step, u):
            send_z(step, [[u[part, near(i), :] for i in range(points)] for part in range(2)],
                   [[u[part, far(i), :] for i in range(points)] for part in range(2)])
            send_x(step, u)

        start = u_ref.at[0]
        for load in loads[:2]:
            load.wait()

        def face_rows(value_of):
            rows = jnp.concatenate([value_of(i) for i in range(points)], axis=0)
            return jnp.concatenate([rows, rows], axis=0).astype(BF16)

        def plane(i, j):
            at = pl.ds(i * face + j * points, points)
            return jnp.concatenate([start[0, at, :], start[1, at, :]], axis=1)

        def slope(i):
            total = None
            for j in range(points):
                term = first_row[j] * plane(i, j)
                total = term if total is None else total + term
            return STRESS_SCALE * total

        wall_rows = lax.broadcasted_iota(jnp.int32, (walls, elements), 0)
        wall_cols = lax.broadcasted_iota(jnp.int32, (walls, elements), 1)
        select = (wall_cols == wall_rows * EY).astype(F32).astype(BF16)
        for j in range(points):
            turn_ref[pl.ds(j * walls, walls), :] = lax.dot_general(
                select, face_rows(lambda i: plane(i, j)), contract, preferred_element_type=F32)
        turn_ref[pl.ds(nodes // 2, walls), :] = lax.dot_general(
            select, face_rows(slope), contract, preferred_element_type=F32)
        for row in range(lane_rows):
            even = turn_ref[pl.ds(2 * row, points, stride=walls), :]
            odd = turn_ref[pl.ds(2 * row + 1, points, stride=walls), :]
            feat_ref[row // 2, :, pl.ds((row % 2) * LANES, LANES)] = jnp.where(low_half, even, odd)
        target = jnp.where(
            low_half,
            turn_ref[pl.ds(nodes // 2, lane_rows, stride=2), :],
            turn_ref[pl.ds(nodes // 2 + 1, lane_rows, stride=2), :],
        )

        pl.semaphore_wait(barrier, learners + groups - 2)
        for offset in range(1, learners):
            remote(count_ref.at[me], count_ref.at[me], count_send.at[offset], count_recv.at[me],
                   {"solver": peer_s(offset)}).start()
        send_faces(0, start)

        def network(first, second, learn):
            turned = jnp.transpose(first).astype(BF16)
            w2_ref[...] = jnp.transpose(jnp.broadcast_to(second, (LANES, width)))

            def one(pair, carry):
                before = jnp.dot(turned, feat_ref[pair].astype(BF16), preferred_element_type=F32)
                hidden = jnp.maximum(before, 0.0)
                if learn:
                    mask_ref[pair] = jnp.where(before > 0.0, 1.0, 0.0).astype(BF16)
                    mixed = jnp.dot(
                        hidden.astype(BF16), graph, preferred_element_type=F32).astype(BF16)
                    mixed_ref[pair] = mixed
                    hidden = mixed.astype(F32)
                weight = w2_ref[...]
                z_ref[pl.ds(2 * pair, 1), :] = jnp.sum(
                    hidden[:, :LANES] * weight, axis=0, keepdims=True)
                z_ref[pl.ds(2 * pair + 1, 1), :] = jnp.sum(
                    hidden[:, LANES:] * weight, axis=0, keepdims=True)
                return carry

            lax.fori_loop(0, pairs, one, 0)
            return z_ref[...]

        output = network(first, second, True)

        for offset in range(1, learners):
            origin = peer_s(offset)
            remote(count_ref.at[me], count_ref.at[origin], count_send.at[offset],
                   count_recv.at[origin], {"solver": origin}).wait_recv()
        counts = count_ref[0]
        for other in range(1, learners):
            counts = counts + count_ref[other]
        inverse = 1.0 / (jnp.maximum(counts, 1.0) * devices)
        places = 2 * lax.broadcasted_iota(jnp.int32, (lane_rows, index_ref.shape[1]), 0)
        chosen = (index_ref[...] == places).astype(F32)
        even = lax.dot_general(chosen, hits, contract, preferred_element_type=F32)
        chosen = (index_ref[...] == places + 1).astype(F32)
        odd = lax.dot_general(chosen, hits, contract, preferred_element_type=F32)
        difference = output - target
        error = jnp.zeros((lane_rows, LANES), F32)
        for learner in range(learners):
            times = jnp.where(low_half, even[:, learner:learner + 1], odd[:, learner:learner + 1])
            single = (difference * inverse[learner:learner + 1]).astype(BF16).astype(F32)
            error = error + times * single
        e_ref[...] = error
        g_ref[...] = lax.dot_general(
            error, small, contract, precision=HIGH, preferred_element_type=F32)

        acc_ref[...] = jnp.zeros_like(acc_ref)
        acc2_ref[...] = jnp.zeros_like(acc2_ref)

        def split(value):
            upper = value.astype(BF16).astype(F32)
            return jnp.concatenate([upper, value - upper], axis=0).astype(BF16)

        def row_pair(ref, pair):
            return jnp.concatenate([ref[pl.ds(2 * pair, 1), :], ref[pl.ds(2 * pair + 1, 1), :]], axis=1)

        def back(pair, carry):
            acc_ref[...] += lax.dot_general(
                split(feat_ref[pair] * row_pair(g_ref, pair)), mask_ref[pair], contract,
                preferred_element_type=F32)
            wide = jnp.broadcast_to(row_pair(e_ref, pair), (8, big))
            acc2_ref[...] += lax.dot_general(
                split(wide), mixed_ref[pair], contract, preferred_element_type=F32)
            return carry

        lax.fori_loop(0, pairs, back, 0)
        grad = acc_ref[0:points, :] + acc_ref[points:2 * points, :]
        grad_second = acc2_ref[0:1, :] + acc2_ref[8:9, :]
        for t in range(owners):
            tile_ref[t, pl.ds(0, points), :] = grad[:, t * owned:(t + 1) * owned]
            tile_ref[t, pl.ds(points, 1), :] = grad_second[:, t * owned:(t + 1) * owned]

        def when_owner(which, action):
            if owners == learners:
                action()
            else:
                pl.when(which < owners)(action)

        def clamp(which):
            return which if owners == learners else jnp.minimum(which, owners - 1)

        def part_copy(offset):
            where = peer_s(offset)
            return where, remote(tile_ref.at[clamp(where)], part_ref.at[me], part_send.at[offset],
                                 part_recv.at[me], {"solver": where})

        for offset in range(1, learners):
            where, copy = part_copy(offset)
            when_owner(where, copy.start)

        def local(source, target, stress):
            u = jnp.concatenate([source[0], source[1]], axis=1)
            upper = u.astype(BF16)
            lower = (u - upper.astype(F32)).astype(BF16)
            u = u + (
                jnp.dot(high_ref[...], upper, preferred_element_type=F32)
                + jnp.dot(high_ref[...], lower, preferred_element_type=F32)
                + jnp.dot(low_ref[...], upper, preferred_element_type=F32)
            )
            for part in range(2):
                target[part] = u[:, part * LANES:(part + 1) * LANES]
            for part in range(2):
                for i in range(points):
                    base = i * face
                    bottom = source[part, pl.ds(base, points), :]
                    top = source[part, pl.ds(base + face - points, points), :]
                    below = jnp.where(level == 0, bottom, roll(top, 1))
                    if stress:
                        below = below + stress_ref[part, pl.ds(i * points, points), :]
                    above = jnp.where(level == EY - 1, 0.0, roll(bottom, -1))
                    target[part, pl.ds(base, points), :] += step_gain * below
                    target[part, pl.ds(base + face - points, points), :] += step_gain * above
            low0 = roll(source[0, pl.ds(nodes - face, face), :], half)
            low1 = roll(source[1, pl.ds(nodes - face, face), :], half)
            target[0, pl.ds(0, face), :] += step_gain_x * jnp.where(low_half, 0.0, low0)
            target[1, pl.ds(0, face), :] += step_gain_x * jnp.where(low_half, low0, low1)
            high0 = roll(source[0, pl.ds(0, face), :], half)
            high1 = roll(source[1, pl.ds(0, face), :], half)
            target[0, pl.ds(nodes - face, face), :] += step_gain * jnp.where(low_half, high0, high1)
            target[1, pl.ds(nodes - face, face), :] += step_gain * jnp.where(low_half, high1, 0.0)
            for part in range(2):
                for i in range(points):
                    before = jnp.where(slot == 0, 0.0, roll(source[part, far(i), :], EY))
                    after = jnp.where(slot == EZL - 1, 0.0, roll(source[part, near(i), :], -EY))
                    target[part, near(i), :] = target[part, near(i), :] + step_gain * before
                    target[part, far(i), :] = target[part, far(i), :] + step_gain * after

        def halo(step, target, send):
            every = copies(step)
            every[0].wait_recv()
            every[1].wait_recv()
            ghost = xr_ref[step, 0]
            ghost = jnp.concatenate([ghost, roll(ghost, half)], axis=0)
            target[0, pl.ds(0, face), :] += step_gain_x * jnp.where(low_half, ghost, 0.0)
            ghost = xr_ref[step, 1]
            ghost = jnp.concatenate([roll(ghost, half), ghost], axis=0)
            target[1, pl.ds(nodes - face, face), :] += step_gain * jnp.where(low_half, 0.0, ghost)
            every[2].wait_recv()
            every[3].wait_recv()
            bottoms, tops = [], []
            for part in range(2):
                before_pack = step_gain * zr_ref[step, 0, part]
                after_pack = step_gain * zr_ref[step, 1, part]
                for i in range(points):
                    before = jnp.where(slot == 0, roll(before_pack, half - EY * i), 0.0)
                    after = jnp.where(
                        slot == EZL - 1, roll(after_pack, EY * (EZL - 1 - i)), 0.0)
                    bottoms.append(target[part, near(i), :] + before)
                    tops.append(target[part, far(i), :] + after)
                    target[part, near(i), :] = bottoms[-1]
                    target[part, far(i), :] = tops[-1]
            if send:
                send_z(step + 1, [bottoms[:points], bottoms[points:]], [tops[:points], tops[points:]])
                send_x(step + 1, target)

        for load in loads[2:]:
            load.wait()
        other = u_ref.at[1]
        local(start, other, False)
        halo(0, other, False)

        def reduce_owned():
            total = tile_ref[clamp(me)]
            for offset in range(1, learners):
                origin = peer_s(offset)
                remote(tile_ref.at[0], part_ref.at[origin], part_send.at[offset],
                       part_recv.at[origin], {"solver": origin}).wait_recv()
            for offset in range(1, learners):
                total = total + part_ref[peer_s(offset)]
            cross_ref[mine] = total
            for offset in range(1, groups):
                remote(cross_ref.at[mine], cross_ref.at[mine], cross_send.at[offset],
                       cross_recv.at[mine], {"group": peer_g(offset)}).start()
            for offset in range(1, groups):
                origin = peer_g(offset)
                remote(cross_ref.at[mine], cross_ref.at[origin], cross_send.at[offset],
                       cross_recv.at[origin], {"group": origin}).wait_recv()
            total = cross_ref[0]
            for origin in range(1, groups):
                total = total + cross_ref[origin]
            at = clamp(me)
            total_ref[at] = total
            for offset in range(1, learners):
                remote(total_ref.at[at], total_ref.at[at], total_send.at[offset],
                       total_recv.at[at], {"solver": peer_s(offset)}).start()

        when_owner(me, reduce_owned)
        for offset in range(1, learners):
            origin = peer_s(offset)
            at = clamp(origin)
            copy = remote(total_ref.at[at], total_ref.at[at], total_send.at[offset],
                          total_recv.at[at], {"solver": origin})
            when_owner(origin, copy.wait_recv)

        sums = jnp.concatenate([total_ref[t] for t in range(owners)], axis=1)
        grad = sums[0:points]
        new_first = (first - LEARN_RATE * (grad * second)).astype(BF16)
        new_second = (second - LEARN_RATE * sums[points:points + 1]).astype(BF16)
        new_first_ref[...] = new_first
        new_second_ref[...] = new_second

        plain = network(new_first.astype(F32), new_second.astype(F32), False)
        stress = jnp.dot(plain, small, precision=HIGH, preferred_element_type=F32)
        stress = jnp.transpose(stress)
        rows_t = 2 * lax.broadcasted_iota(jnp.int32, (lane_rows, elements), 0)
        cols_t = lax.broadcasted_iota(jnp.int32, (lane_rows, elements), 1)
        placed = jnp.dot(
            stress[:face], (cols_t == rows_t * EY).astype(F32),
            precision=HIGH, preferred_element_type=F32,
        ) + jnp.dot(
            stress[face:], (cols_t == (rows_t + 1) * EY).astype(F32),
            precision=HIGH, preferred_element_type=F32,
        )
        for part in range(2):
            columns = placed[:, part * LANES:(part + 1) * LANES]
            stress_ref[part] = columns
            for i in range(points):
                other[part, pl.ds(i * face, points), :] += (
                    step_gain * columns[i * points:(i + 1) * points])

        if FLOW_STEPS > 1:
            send_faces(1, other)
        held = [start, other]
        for step in range(1, FLOW_STEPS):
            final = step == FLOW_STEPS - 1
            source, target = held[step % 2], out_ref if final else held[(step + 1) % 2]
            local(source, target, True)
            halo(step, target, not final)

        for offset in range(1, learners):
            remote(count_ref.at[me], count_ref.at[me], count_send.at[offset], count_recv.at[me],
                   {"solver": peer_s(offset)}).wait_send()
            where, copy = part_copy(offset)
            when_owner(where, copy.wait_send)

        def drain_owned():
            at = clamp(me)
            for offset in range(1, groups):
                remote(cross_ref.at[mine], cross_ref.at[mine], cross_send.at[offset],
                       cross_recv.at[mine], {"group": peer_g(offset)}).wait_send()
            for offset in range(1, learners):
                remote(total_ref.at[at], total_ref.at[at], total_send.at[offset],
                       total_recv.at[at], {"solver": peer_s(offset)}).wait_send()

        when_owner(me, drain_owned)
        for step in range(FLOW_STEPS):
            for copy in copies(step):
                copy.wait_send()

    dma = pltpu.SemaphoreType.DMA
    scratch = [
        pltpu.VMEM((2, 2, nodes, LANES), F32),
        pltpu.VMEM((nodes, nodes), BF16),
        pltpu.VMEM((nodes, nodes), BF16),
        pltpu.VMEM((pairs, width, 2 * LANES), BF16),
        pltpu.VMEM((pairs, width, 2 * LANES), BF16),
        pltpu.VMEM((pairs, points, 2 * LANES), F32),
        pltpu.VMEM((nodes // 2 + walls, LANES), F32),
        pltpu.VMEM((lane_rows, LANES), F32),
        pltpu.VMEM((lane_rows, LANES), F32),
        pltpu.VMEM((lane_rows, LANES), F32),
        pltpu.VMEM((width, LANES), F32),
        pltpu.VMEM((2 * points, width), F32),
        pltpu.VMEM((16, width), F32),
        pltpu.VMEM((learners, learners, LANES), F32),
        pltpu.VMEM((owners, rows_sent, owned), F32),
        pltpu.VMEM((learners, rows_sent, owned), F32),
        pltpu.VMEM((groups, rows_sent, owned), F32),
        pltpu.VMEM((owners, rows_sent, owned), F32),
        pltpu.VMEM((2, face, LANES), F32),
        pltpu.VMEM((FLOW_STEPS, 2, face // 2, LANES), F32),
        pltpu.VMEM((FLOW_STEPS, 2, face // 2, LANES), F32),
        pltpu.VMEM((FLOW_STEPS, 2, 2, points, LANES), F32),
        pltpu.VMEM((FLOW_STEPS, 2, 2, points, LANES), F32),
        dma((4,)),
        dma((learners,)), dma((learners,)), dma((learners,)), dma((learners,)),
        dma((groups,)), dma((groups,)), dma((learners,)), dma((owners,)),
        dma((FLOW_STEPS, 2)), dma((FLOW_STEPS, 2)), dma((FLOW_STEPS, 2)), dma((FLOW_STEPS, 2)),
    ]
    return kernel, scratch


def store_kernel(field_ref, first_ref, second_ref, field_out, first_out, second_out, sem):
    copies = [
        pltpu.make_async_copy(
            field_ref.at[part], field_out.at[:, pl.ds(part * LANES, LANES)], sem.at[part])
        for part in range(2)
    ]
    copies.append(pltpu.make_async_copy(first_ref, first_out, sem.at[2]))
    copies.append(pltpu.make_async_copy(second_ref, second_out, sem.at[3]))
    for copy in copies:
        copy.start()
    for copy in copies:
        copy.wait()


def shards(field, first_weight, second_weight, face_edges, sample_index, route):
    points = field.shape[0]
    elements = field.shape[3]
    nodes = points**3
    width = first_weight.shape[1]
    learners = lax.axis_size("solver")
    groups = lax.axis_size("group")
    deriv, end_weight = gll_tables(points)
    gain = 2.0 / end_weight
    high, low = element_operator(deriv, gain)
    kernel, scratch = make_kernel(learners, groups, points, width, deriv, gain)
    vmem = pl.BlockSpec(memory_space=pltpu.VMEM)
    hbm = pl.BlockSpec(memory_space=pltpu.HBM)
    results = pl.pallas_call(
        kernel,
        out_shape=(
            jax.ShapeDtypeStruct((2, nodes, LANES), F32),
            jax.ShapeDtypeStruct(first_weight.shape, BF16),
            jax.ShapeDtypeStruct((1, width), BF16),
        ),
        in_specs=[hbm] + [vmem] * 5 + [hbm] * 2,
        out_specs=(vmem, vmem, vmem),
        scratch_shapes=scratch,
        compiler_params=pltpu.CompilerParams(
            collective_id=0, has_side_effects=True, vmem_limit_bytes=48 * 1024 * 1024
        ),
        name="step",
    )(
        field.reshape(nodes, elements),
        first_weight,
        second_weight.reshape(1, width),
        face_edges,
        sample_index.reshape(1, -1),
        route.reshape(1, -1),
        jnp.asarray(high),
        jnp.asarray(low),
    )
    new_field, new_first, new_second = pl.pallas_call(
        store_kernel,
        out_shape=(
            jax.ShapeDtypeStruct((nodes, elements), F32),
            jax.ShapeDtypeStruct(first_weight.shape, BF16),
            jax.ShapeDtypeStruct((1, width), BF16),
        ),
        in_specs=[vmem] * 3,
        out_specs=(hbm, hbm, hbm),
        scratch_shapes=[pltpu.SemaphoreType.DMA((4,))],
        name="store",
    )(*results)
    return (new_field.reshape(field.shape), new_first, new_second.reshape(second_weight.shape))


def solution(mesh):
    return jax.shard_map(
        shards,
        mesh=mesh,
        in_specs=(
            P(None, None, None, ("solver", "group")),
            P(),
            P(),
            P(),
            P(("solver", "group")),
            P(("solver", "group"), None),
        ),
        out_specs=(P(None, None, None, ("solver", "group")), P(), P()),
        check_vma=False,
    )
```

time: 49.7 us -> 52.9 us (1.064)
  Pallas kernels: 42.2 us -> 45.3 us
    pallas_call x1 -> x2, Pallas kernels: 42.2 us -> 45.3 us  [the longest x1 43.5 us: shards(): pl.pallas_call(kernel, out_shape=(jax.ShapeDtypeStruct((2, nodes, LANES),...]
    unnamed x19 -> x22, local copies, waits for them, and re-layouts: 6.5 us -> 6.48 us
where the time goes in v2:
time: 52.9 us; the launch traced here: 52.5 us
  Pallas kernels  45.3 us (86%)
  local copies, waits for them, and re-layouts  6.48 us (12%)
  between operations  0.69 us (1%)
    pallas_call x1, Pallas kernels, shards(): pl.pallas_call(kernel, out_shape=(jax.ShapeDtypeStruct((2, nodes, LANES),...  43.5 us
    unnamed x22, local copies, waits for them, and re-layouts  6.48 us
    pallas_call x1, Pallas kernels, shards(): pl.pallas_call(store_kernel, out_shape=(jax.ShapeDtypeStruct((nodes, elem...  1.89 us

profile of v2, /device:TPU:0, one launch (start us, length us, event | category | flops | bytes accessed | tf_op | source)
XLA Modules:
  0.0 52.5 jit_solution(14317899967343226493)
XLA Ops:
  0.6 0.0 copy-start.6
  0.6 0.0 copy-start.8
  0.7 0.0 copy-start.9
  0.7 0.0 copy-start.10
  0.7 0.6 %copy-done.6 = bf16[1024,1]{0,1:T(2,128)(2,1)S(1)} copy-done((bf16[1024,1]{0,1:T(2,128)(2,1)S(1)}, bf16[1024,1]{0,1:T(2,128)(2,1)}, u32[]{:S(2)}) %copy-start.6) | copy-done | bytes 2072
  1.3 0.0 copy-done.8
  1.3 0.0 copy-done.9
  1.3 0.0 copy-done.10
  1.3 0.0 copy-start
  1.3 1.0 %copy-done = f32[8,8,8,256]{3,2,1,0:T(8,128)S(1)} copy-done((f32[8,8,8,256]{3,2,1,0:T(8,128)S(1)}, f32[8,8,8,256]{3,2,1,0:T(8,128)}, u32[]{:S(2)}) %copy-start) | copy-done | bytes 524312
  2.4 0.0 copy-start.1
  2.4 1.0 %copy-done.1 = bf16[512,512]{1,0:T(8,128)(2,1)S(1)} copy-done((bf16[512,512]{1,0:T(8,128)(2,1)S(1)}, bf16[512,512]{1,0:T(8,128)(2,1)}, u32[]{:S(2)}) %copy-start.1) | copy-done | bytes 524312
  3.4 0.0 copy-start.3
  3.4 1.0 %copy-done.3 = bf16[512,512]{1,0:T(8,128)(2,1)S(1)} copy-done((bf16[512,512]{1,0:T(8,128)(2,1)S(1)}, bf16[512,512]{1,0:T(8,128)(2,1)}, u32[]{:S(2)}) %copy-start.3) | copy-done | bytes 524312
  4.5 0.0 copy-start.4
  4.5 0.7 %copy-done.4 = bf16[8,1024]{1,0:T(8,128)(2,1)S(1)} copy-done((bf16[8,1024]{1,0:T(8,128)(2,1)S(1)}, bf16[8,1024]{1,0:T(8,128)(2,1)}, u32[]{:S(2)}) %copy-start.4) | copy-done | bytes 16408
  5.2 43.5 %step.1 = (f32[2,512,128]{2,1,0:T(8,128)S(1)}, bf16[8,1024]{1,0:T(8,128)(2,1)S(1)}, bf16[1,1024]{1,0:T(2,128)(2,1)S(1)}) custom-call(f32[512,256]{1,0:T(8,128)S(1)} %bitcast.6, bf16[8,1024]{1,0:T(8,128)(2,1)S(1)} %copy-done.4, bf16[1,1024]{1,0:T(2,128)(2,1)S(1)} %bitcast.7, s32[2,256]{1,0:T(2,128)S(1)} %copy-done.8, s32[1,64]{1,0:T(1,128)S(1)} %bitcast.8, ...), custom_call_target="tpu_custom_call" | custom-call | tf_op jit(solution)/shard_map/step/pallas_call | solution.py:576
  48.6 0.0 copy-start.2
  48.7 0.8 %copy-done.2 = f32[2,512,128]{2,1,0:T(8,128)} copy-done((f32[2,512,128]{2,1,0:T(8,128)}, f32[2,512,128]{2,1,0:T(8,128)S(1)}, u32[]{:S(2)}) %copy-start.2) | copy-done | bytes 524312
  49.4 0.0 copy-start.5
  49.5 0.6 %copy-done.5 = bf16[8,1024]{1,0:T(8,128)(2,1)} copy-done((bf16[8,1024]{1,0:T(8,128)(2,1)}, bf16[8,1024]{1,0:T(8,128)(2,1)S(1)}, u32[]{:S(2)}) %copy-start.5) | copy-done | bytes 16408
  50.0 0.0 copy-start.7
  50.0 0.6 %copy-done.7 = bf16[1,1024]{1,0:T(2,128)(2,1)} copy-done((bf16[1,1024]{1,0:T(2,128)(2,1)}, bf16[1,1024]{1,0:T(2,128)(2,1)S(1)}, u32[]{:S(2)}) %copy-start.7) | copy-done | bytes 2072
  50.6 1.9 %store.1 = (f32[512,256]{1,0:T(8,128)}, bf16[8,1024]{1,0:T(8,128)(2,1)}, bf16[1,1024]{1,0:T(2,128)(2,1)}) custom-call(f32[2,512,128]{2,1,0:T(8,128)} %copy-done.2, bf16[8,1024]{1,0:T(8,128)(2,1)} %copy-done.5, bf16[1,1024]{1,0:T(2,128)(2,1)} %copy-done.7), custom_call_target="tpu_custom_call" | custom-call | tf_op jit(solution)/shard_map/store/pallas_call | solution.py:600
Async XLA Ops:
  0.6 0.7 %copy-start.6 = (bf16[1024,1]{0,1:T(2,128)(2,1)S(1)}, bf16[1024,1]{0,1:T(2,128)(2,1)}, u32[]{:S(2)}) copy-start(bf16[1024,1]{0,1:T(2,128)(2,1)} %param.10) | copy-start | bytes 6148
  0.6 0.7 %copy-start.8 = (s32[2,256]{1,0:T(2,128)S(1)}, s32[2,256]{1,0:T(2,128)}, u32[]{:S(2)}) copy-start(s32[2,256]{1,0:T(2,128)} %edges_ref.1) | copy-start | bytes 6148
  0.7 0.7 %copy-start.9 = (s32[64]{0:T(128)S(1)}, s32[64]{0:T(128)}, u32[]{:S(2)}) copy-start(s32[64]{0:T(128)} %param.12) | copy-start | bytes 772
  0.7 0.7 %copy-start.10 = (s32[64,1]{0,1:T(1,128)S(1)}, s32[64,1]{0,1:T(1,128)}, u32[]{:S(2)}) copy-start(s32[64,1]{0,1:T(1,128)} %param.13) | copy-start | bytes 772
  1.3 1.0 %copy-start = (f32[8,8,8,256]{3,2,1,0:T(8,128)S(1)}, f32[8,8,8,256]{3,2,1,0:T(8,128)}, u32[]{:S(2)}) copy-start(f32[8,8,8,256]{3,2,1,0:T(8,128)} %param.8) | copy-start | bytes 1572868
  2.4 1.0 %copy-start.1 = (bf16[512,512]{1,0:T(8,128)(2,1)S(1)}, bf16[512,512]{1,0:T(8,128)(2,1)}, u32[]{:S(2)}) copy-start(bf16[512,512]{1,0:T(8,128)(2,1)} %constant.5.clone.low_hbm) | copy-start | bytes 1572868
  3.4 1.0 %copy-start.3 = (bf16[512,512]{1,0:T(8,128)(2,1)S(1)}, bf16[512,512]{1,0:T(8,128)(2,1)}, u32[]{:S(2)}) copy-start(bf16[512,512]{1,0:T(8,128)(2,1)} %constant.4.clone.high_hbm) | copy-start | bytes 1572868
  4.5 0.7 %copy-start.4 = (bf16[8,1024]{1,0:T(8,128)(2,1)S(1)}, bf16[8,1024]{1,0:T(8,128)(2,1)}, u32[]{:S(2)}) copy-start(bf16[8,1024]{1,0:T(8,128)(2,1)} %first_ref.1) | copy-start | bytes 49156
  48.6 0.8 %copy-start.2 = (f32[2,512,128]{2,1,0:T(8,128)}, f32[2,512,128]{2,1,0:T(8,128)S(1)}, u32[]{:S(2)}) copy-start(f32[2,512,128]{2,1,0:T(8,128)S(1)} %get-tuple-element.9.field_ref) | copy-start | bytes 1572868
  49.4 0.6 %copy-start.5 = (bf16[8,1024]{1,0:T(8,128)(2,1)}, bf16[8,1024]{1,0:T(8,128)(2,1)S(1)}, u32[]{:S(2)}) copy-start(bf16[8,1024]{1,0:T(8,128)(2,1)S(1)} %get-tuple-element.10.first_ref) | copy-start | bytes 49156
  50.0 0.6 %copy-start.7 = (bf16[1,1024]{1,0:T(2,128)(2,1)}, bf16[1,1024]{1,0:T(2,128)(2,1)S(1)}, u32[]{:S(2)}) copy-start(bf16[1,1024]{1,0:T(2,128)(2,1)S(1)} %get-tuple-element.11.second_ref) | copy-start | bytes 6148

commit v3 on v2

--- a/solution.py
+++ b/solution.py
@@ -244,7 +244,7 @@
         for j in range(points):
             turn_ref[pl.ds(j * walls, walls), :] = lax.dot_general(
                 select, face_rows(lambda i: plane(i, j)), contract, preferred_element_type=F32)
-        turn_ref[pl.ds(nodes // 2, walls), :] = lax.dot_general(
+        turn_ref[pl.ds(points * walls, walls), :] = lax.dot_general(
             select, face_rows(slope), contract, preferred_element_type=F32)
         for row in range(lane_rows):
             even = turn_ref[pl.ds(2 * row, points, stride=walls), :]
@@ -252,8 +252,8 @@
             feat_ref[row // 2, :, pl.ds((row % 2) * LANES, LANES)] = jnp.where(low_half, even, odd)
         target = jnp.where(
             low_half,
-            turn_ref[pl.ds(nodes // 2, lane_rows, stride=2), :],
-            turn_ref[pl.ds(nodes // 2 + 1, lane_rows, stride=2), :],
+            turn_ref[pl.ds(points * walls, lane_rows, stride=2), :],
+            turn_ref[pl.ds(points * walls + 1, lane_rows, stride=2), :],
         )
 
         pl.semaphore_wait(barrier, learners + groups - 2)
@@ -489,9 +489,11 @@
         held = [start, other]
         for step in range(1, FLOW_STEPS):
             final = step == FLOW_STEPS - 1
-            source, target = held[step % 2], out_ref if final else held[(step + 1) % 2]
+            source, target = held[step % 2], held[(step + 1) % 2]
             local(source, target, True)
             halo(step, target, not final)
+        for part in range(2):
+            out_ref[:, part * LANES:(part + 1) * LANES] = held[FLOW_STEPS % 2][part]
 
         for offset in range(1, learners):
             remote(count_ref.at[me], count_ref.at[me], count_send.at[offset], count_recv.at[me],
@@ -521,7 +523,7 @@
         pltpu.VMEM((pairs, width, 2 * LANES), BF16),
         pltpu.VMEM((pairs, width, 2 * LANES), BF16),
         pltpu.VMEM((pairs, points, 2 * LANES), F32),
-        pltpu.VMEM((nodes // 2 + walls, LANES), F32),
+        pltpu.VMEM((points * walls + walls, LANES), F32),
         pltpu.VMEM((lane_rows, LANES), F32),
         pltpu.VMEM((lane_rows, LANES), F32),
         pltpu.VMEM((lane_rows, LANES), F32),
@@ -546,20 +548,6 @@
     return kernel, scratch
 
 
-def store_kernel(field_ref, first_ref, second_ref, field_out, first_out, second_out, sem):
-    copies = [
-        pltpu.make_async_copy(
-            field_ref.at[part], field_out.at[:, pl.ds(part * LANES, LANES)], sem.at[part])
-        for part in range(2)
-    ]
-    copies.append(pltpu.make_async_copy(first_ref, first_out, sem.at[2]))
-    copies.append(pltpu.make_async_copy(second_ref, second_out, sem.at[3]))
-    for copy in copies:
-        copy.start()
-    for copy in copies:
-        copy.wait()
-
-
 def shards(field, first_weight, second_weight, face_edges, sample_index, route):
     points = field.shape[0]
     elements = field.shape[3]
@@ -573,10 +561,10 @@
     kernel, scratch = make_kernel(learners, groups, points, width, deriv, gain)
     vmem = pl.BlockSpec(memory_space=pltpu.VMEM)
     hbm = pl.BlockSpec(memory_space=pltpu.HBM)
-    results = pl.pallas_call(
+    new_field, new_first, new_second = pl.pallas_call(
         kernel,
         out_shape=(
-            jax.ShapeDtypeStruct((2, nodes, LANES), F32),
+            jax.ShapeDtypeStruct((nodes, elements), F32),
             jax.ShapeDtypeStruct(first_weight.shape, BF16),
             jax.ShapeDtypeStruct((1, width), BF16),
         ),
@@ -584,7 +572,7 @@
         out_specs=(vmem, vmem, vmem),
         scratch_shapes=scratch,
         compiler_params=pltpu.CompilerParams(
-            collective_id=0, has_side_effects=True, vmem_limit_bytes=48 * 1024 * 1024
+            collective_id=0, has_side_effects=True, vmem_limit_bytes=67_043_328
         ),
         name="step",
     )(
@@ -597,18 +585,6 @@
         jnp.asarray(high),
         jnp.asarray(low),
     )
-    new_field, new_first, new_second = pl.pallas_call(
-        store_kernel,
-        out_shape=(
-            jax.ShapeDtypeStruct((nodes, elements), F32),
-            jax.ShapeDtypeStruct(first_weight.shape, BF16),
-            jax.ShapeDtypeStruct((1, width), BF16),
-        ),
-        in_specs=[vmem] * 3,
-        out_specs=(hbm, hbm, hbm),
-        scratch_shapes=[pltpu.SemaphoreType.DMA((4,))],
-        name="store",
-    )(*results)
     return (new_field.reshape(field.shape), new_first, new_second.reshape(second_weight.shape))
 
 

time: 52.9 us -> 49 us (0.926)
  local copies, waits for them, and re-layouts: 6.48 us -> 3.15 us
    unnamed x22 -> x7, local copies, waits for them, and re-layouts: 6.48 us -> 3.15 us
    pallas_call x2 -> x1, Pallas kernels: 45.3 us -> 44.9 us  [shards(): pl.pallas_call(kernel, out_shape=(jax.ShapeDtypeStruct((nodes, elements),...]
where the time goes in v3:
time: 49 us; the launch traced here: 48.8 us
  Pallas kernels  44.9 us (92%)
  local copies, waits for them, and re-layouts  3.15 us (6%)
  between operations  0.65 us (1%)
    pallas_call x1, Pallas kernels, shards(): pl.pallas_call(kernel, out_shape=(jax.ShapeDtypeStruct((nodes, elements),...  44.9 us
    unnamed x7, local copies, waits for them, and re-layouts  3.15 us

profile of v3, /device:TPU:0, one launch (start us, length us, event | category | flops | bytes accessed | tf_op | source)
XLA Modules:
  0.0 48.8 jit_solution(3117379712741897891)
XLA Ops:
  0.6 44.9 %step.1 = (f32[512,256]{1,0:T(8,128)}, bf16[8,1024]{1,0:T(8,128)(2,1)}, bf16[1,1024]{1,0:T(2,128)(2,1)}) custom-call(f32[512,256]{1,0:T(8,128)} %bitcast.6, bf16[8,1024]{1,0:T(8,128)(2,1)} %first_ref.1, bf16[1,1024]{1,0:T(2,128)(2,1)} %bitcast.8, s32[2,256]{1,0:T(2,128)} %edges_ref.1, s32[1,64]{1,0:T(1,128)} %bitcast.10, s32[1,64]{1,0:T(1,128)} %bitcast.11, ...), custom_call_target="tpu_custom_call" | custom-call | tf_op jit(solution)/shard_map/step/pallas_call | solution.py:564
  45.6 0.0 copy-start
  45.6 1.9 %copy.14 = f32[8,8,8,256]{3,2,1,0:T(8,128)} copy(f32[8,8,8,256]{3,2,1,0:T(8,128)} %bitcast.7) | data formatting | bytes 1048576
  47.5 0.0 copy-done
  47.5 0.0 copy-start.1
  47.5 0.6 %copy.15 = bf16[8,1024]{1,0:T(8,128)(2,1)} copy(bf16[8,1024]{1,0:T(8,128)(2,1)S(1)} %copy-done) | data formatting | bytes 32768
  48.1 0.1 copy-done.1
  48.2 0.6 %copy.16 = bf16[1024,1]{0,1:T(2,128)(2,1)} copy(bf16[1024,1]{0,1:T(2,128)(2,1)S(1)} %bitcast.9) | data formatting | bytes 4096
Async XLA Ops:
  45.6 1.9 %copy-start = (bf16[8,1024]{1,0:T(8,128)(2,1)S(1)}, bf16[8,1024]{1,0:T(8,128)(2,1)}, u32[]{:S(2)}) copy-start(bf16[8,1024]{1,0:T(8,128)(2,1)} %get-tuple-element.13) | copy-start | bytes 49156
  47.5 0.7 %copy-start.1 = (bf16[1,1024]{1,0:T(2,128)(2,1)S(1)}, bf16[1,1024]{1,0:T(2,128)(2,1)}, u32[]{:S(2)}) copy-start(bf16[1,1024]{1,0:T(2,128)(2,1)} %get-tuple-element.8) | copy-start | bytes 6148
